TPU v7x, 512 devices: a whole 4x8x8 slice. The times are simulated.
512 devices in a mesh: tok: 64 (over x, z, core), head: 8 (over y).
Axes of the slice: x: 4, y: 8, z: 8, core: 2. Of those that a mesh axis runs over, the one named last changes fastest.
Arguments:
- qkv: bfloat16 [3, 16384, 3072], P(None, 'tok', 'head'), may hold values from -8 to 8
- token_rank: int32 [48, 16384], P('head', 'tok'), may hold values from 0 to 16383, as said below
- cluster_sizes: int32 [48, 256], P('head'), may hold values from 1 to 381, as said below
- cluster_owner: int32 [48, 256], P('head'), may hold values from 0 to 63, as said below
- cache_zero: bfloat16 [16384, 3072], P('tok', 'head'), may hold values from -1.796875 to 1.796875
- cache_one: bfloat16 [16384, 3072], P('tok', 'head'), may hold values from -1.796875 to 1.796875
- cache_two: bfloat16 [16384, 3072], P('tok', 'head'), may hold values from -1.796875 to 1.796875
- cache_uncond: bfloat16 [16384, 3072], P('tok', 'head'), may hold values from -4 to 4
- norm_gain: float32 [3072], replicated, may hold values from 0.5 to 1.5
- norm_bias: float32 [3072], replicated, may hold values from -3 to 3
Outputs:
- normed: bfloat16 [16384, 3072], P(('tok', 'head'))
- taylor_zero: bfloat16 [16384, 3072], P('tok', 'head')
- taylor_one: bfloat16 [16384, 3072], P('tok', 'head')
- taylor_two: bfloat16 [16384, 3072], P('tok', 'head')
- taylor_three: bfloat16 [16384, 3072], P('tok', 'head')
Inputs may be any that keep to these rules, and one draw needn't show every extreme that they name: `token_rank`: for each head a permutation of the tokens: the position of each token when the tokens are ordered by cluster, clusters in increasing number. `cluster_sizes`: for each head the sizes sum to 16384; every head has a cluster of exactly 381 tokens. `cluster_owner`: each group holds 4 clusters of every head and at most 384 tokens of a head, a bound that some group of every head reaches; of the tokens that one index of tok holds, at most 8 of one head lie in one group, a bound reached in every draw; heads 2j and 2j + 1 together have exactly 8 of those tokens in each group.
All inputs are finite; a program needn't handle non-finite values.
Results may differ from a plain program's by a relative error of at most 0.0059.
Values may be sent and summed in bfloat16 or wider, within the bound.
No kernel may reach another device: no remote copies, remote signals or barrier semaphores. Data moves between devices by JAX's collectives and lax.ppermute only.
A program may use at most 64 MiB of HBM per device.

v0:
```python
import math

import jax
import jax.numpy as jnp
from jax import lax
from jax.sharding import Mesh
from jax.sharding import PartitionSpec as P

HEAD_DIM = 64
STEP_GAP = 2
TOK = ("tok_0", "tok_1", "tok_2")
TOK_HEAD = ("tok_0", "tok_1", "tok_2", "head")


guide_scale = 6.0
norm_eps = 1e-05


def side_by_side(arrays, axis, split_dim, concat_dim, along):
    widths = [a.shape[along] for a in arrays]
    both = jnp.concatenate(arrays, axis=along)
    filled = lax.all_to_all(both, axis, split_axis=split_dim, concat_axis=concat_dim, tiled=True)
    return tuple(jnp.split(filled, [sum(widths[:k]) for k in range(1, len(widths))], axis=along))


def in_blocks(value, dim, size):
    lengths = value.shape
    tiles = value.reshape(*lengths[:dim], size, lengths[dim] // size, *lengths[dim + 1 :])
    return jnp.moveaxis(tiles, dim, 0)


def in_order(tiles, dim):
    lengths = list(tiles.shape[1:])
    lengths[dim] *= tiles.shape[0]
    return jnp.moveaxis(tiles, 0, dim).reshape(lengths)


def exchange_in_order(tiles, axes, order):
    lengths = [lax.axis_size(a) for a in axes]
    tiles = tiles.reshape(*lengths, *tiles.shape[1:])
    for k in order:
        tiles = lax.all_to_all(tiles, axes[k], split_axis=k, concat_axis=k, tiled=True)
    return tiles.reshape(-1, *tiles.shape[len(axes) :])


def two_step_exchange(value, groups, order, split_dim, concat_dim):
    size = lax.axis_size(groups[0]) * lax.axis_size(groups[1])
    tiles = in_blocks(value, split_dim, size)
    return in_order(exchange_in_order(tiles, groups, order), concat_dim)


def attend_pool(query_rows, key_rows, value_rows, tag_rows):
    total_rows = query_rows.shape[0]
    block_rows = math.gcd(total_rows, 512)

    def one_block(begin):
        block_q = lax.dynamic_slice_in_dim(query_rows, begin, block_rows, 0)
        block_tags = lax.dynamic_slice_in_dim(tag_rows, begin, block_rows, 0)
        scores = lax.dot_general(
            block_q, key_rows, (((1,), (1,)), ((), ())), preferred_element_type=jnp.float32
        ) * (1.0 / math.sqrt(HEAD_DIM))
        allowed = block_tags[:, None] == tag_rows[None, :]
        masked = jnp.where(allowed, scores, -jnp.inf)
        largest = jnp.max(masked, axis=1, keepdims=True)
        expo = jnp.where(allowed, jnp.exp(masked - largest), 0.0)
        totals = jnp.sum(expo, axis=1, keepdims=True)
        probability = (expo / totals).astype(jnp.bfloat16)
        return jnp.dot(probability, value_rows, preferred_element_type=jnp.float32).astype(
            jnp.bfloat16
        )

    starts = jnp.arange(total_rows // block_rows, dtype=jnp.int32) * block_rows
    return lax.map(one_block, starts).reshape(total_rows, HEAD_DIM)


def taylor_terms(attention, cache_zero, cache_one, cache_two):
    first_diff = (attention.astype(jnp.float32) - cache_zero.astype(jnp.float32)) / STEP_GAP
    second_diff = (first_diff - cache_one.astype(jnp.float32)) / STEP_GAP
    third_diff = (second_diff - cache_two.astype(jnp.float32)) / STEP_GAP
    return (
        first_diff.astype(jnp.bfloat16),
        second_diff.astype(jnp.bfloat16),
        third_diff.astype(jnp.bfloat16),
    )


def guide_rows(attention, cache_uncond):
    attention_wide = attention.astype(jnp.float32)
    uncond_wide = cache_uncond.astype(jnp.float32)
    return (uncond_wide + guide_scale * (attention_wide - uncond_wide)).astype(jnp.bfloat16)


def layer_norm(guided, norm_gain, norm_bias):
    widened = lax.optimization_barrier(guided).astype(jnp.float32)
    row_mean = jnp.mean(widened, axis=1, keepdims=True)
    centered = widened - row_mean
    row_var = jnp.mean(centered * centered, axis=1, keepdims=True)
    return (centered * lax.rsqrt(row_var + norm_eps) * norm_gain + norm_bias).astype(jnp.bfloat16)


def on_device(
    qkv,
    token_rank,
    cluster_sizes,
    cluster_owner,
    cache_zero,
    cache_one,
    cache_two,
    cache_uncond,
    norm_gain,
    norm_bias,
):
    group_count = lax.axis_size(TOK)
    head_count = token_rank.shape[0]
    tok_count = token_rank.shape[1]
    cluster_count = cluster_sizes.shape[1]
    cluster_ends = jnp.cumsum(cluster_sizes, axis=1)
    members = jnp.sum(
        (cluster_ends[:, None, :] <= token_rank[:, :, None]).astype(jnp.int32), axis=2
    )
    chosen = members[:, :, None] == jnp.arange(cluster_count, dtype=jnp.int32)[None, None, :]
    targets = jnp.sum(jnp.where(chosen, cluster_owner[:, None, :], 0), axis=2)
    dest_hits = (
        targets[:, :, None] == jnp.arange(group_count, dtype=jnp.int32)[None, None, :]
    ).astype(jnp.int32)
    earlier = jnp.cumsum(dest_hits, axis=1) - dest_hits
    position = jnp.sum(earlier * dest_hits, axis=2)
    head_ids = jnp.arange(head_count, dtype=jnp.int32)[:, None]
    flat_id = (jnp.arange(tok_count, dtype=jnp.int32)[None, :] * head_count + head_ids).reshape(-1)
    query_flat = qkv[0].reshape(tok_count * head_count, HEAD_DIM)
    key_flat = qkv[1].reshape(tok_count * head_count, HEAD_DIM)
    value_flat = qkv[2].reshape(tok_count * head_count, HEAD_DIM)
    pool = head_count * (tok_count // group_count)
    group_counts = jnp.sum(dest_hits, axis=1)
    head_offset = jnp.cumsum(group_counts, axis=0) - group_counts
    base_offset = jnp.take_along_axis(head_offset, targets, axis=1)
    pool_index = targets * pool + base_offset + position
    pool_source = (
        jnp.zeros((group_count * pool,), jnp.int32).at[pool_index.reshape(-1)].set(flat_id)
    )
    tag_values = (head_ids * cluster_count + members).reshape(-1)
    pool_tags = (
        jnp.zeros((group_count * pool,), jnp.int32).at[pool_index.reshape(-1)].set(tag_values)
    )
    send_q = query_flat[pool_source].reshape(group_count, pool * HEAD_DIM)
    send_k = key_flat[pool_source].reshape(group_count, pool * HEAD_DIM)
    send_v = value_flat[pool_source].reshape(group_count, pool * HEAD_DIM)
    arrived = (
        *side_by_side((send_q, send_k, send_v), TOK, 0, 0, 1),
        lax.all_to_all(
            pool_tags.reshape(group_count, pool), TOK, split_axis=0, concat_axis=0, tiled=True
        ),
    )
    pooled = attend_pool(
        arrived[0].reshape(group_count * pool, HEAD_DIM),
        arrived[1].reshape(group_count * pool, HEAD_DIM),
        arrived[2].reshape(group_count * pool, HEAD_DIM),
        arrived[3].reshape(-1),
    )
    back_pool = two_step_exchange(
        pooled.reshape(group_count, pool * HEAD_DIM), (("tok_0", "tok_1"), "tok_2"), (1, 0), 0, 0
    )
    picked = back_pool.reshape(group_count * pool, HEAD_DIM)[pool_index.transpose(1, 0).reshape(-1)]
    attention = picked.reshape(tok_count, head_count * HEAD_DIM)
    first_cols, second_cols, third_cols = taylor_terms(attention, cache_zero, cache_one, cache_two)
    guided = guide_rows(attention, cache_uncond)
    whole_rows = lax.all_to_all(guided, "head", split_axis=0, concat_axis=1, tiled=True)
    normed = layer_norm(whole_rows, norm_gain, norm_bias)
    return (normed, attention, first_cols, second_cols, third_cols)


def solution(mesh):
    torus = Mesh(
        mesh.devices.reshape(4, 8, 2, mesh.shape["head"]), ("tok_0", "tok_1", "tok_2", "head")
    )
    in_specs = (
        P(None, TOK, "head"),
        P("head", TOK),
        P("head", None),
        P("head", None),
        P(TOK, "head"),
        P(TOK, "head"),
        P(TOK, "head"),
        P(TOK, "head"),
        P(),
        P(),
    )
    out_specs = (P(TOK_HEAD, None), P(TOK, "head"), P(TOK, "head"), P(TOK, "head"), P(TOK, "head"))
    return jax.shard_map(
        on_device, mesh=torus, in_specs=in_specs, out_specs=out_specs, check_vma=False
    )
```

profile of v0, /device:TPU:6, one launch (start us, length us, event | category | flops | bytes accessed | tf_op | source)
XLA Modules:
  0.0 148.2 jit_solution(2691122211074162519)
XLA Ops:
  0.6 0.7 reshape.248
  1.3 1.8 %reduce-window.14 = s32[6,2,128]{2,1,0:T(2,128)S(1)} reduce-window(s32[6,2,128]{2,1,0:T(2,128)S(1)} %reshape.248, s32[]{:T(128)} %constant.35.clone.1), window={size=1x1x128 pad=0_0x0_0x127_0}, to_apply=%region_0.0 | reduce-window | flops 195072 | bytes 12292 | tf_op jit(solution)/shard_map/reduce-window
  3.2 0.1 copy.54
  3.4 0.1 copy.55
  3.6 1.2 convert_reduce_fusion
  4.8 1.2 select_reduce_fusion
  6.1 3.6 %reduce-window.16 = s32[6,64,2,128]{3,1,2,0:T(8,128)S(1)} reduce-window(s32[6,64,2,128]{3,1,2,0:T(8,128)S(1)} %fusion.19, s32[]{:T(128)} %constant.35.clone.1), window={size=1x1x1x128 pad=0_0x0_0x0_0x127_0}, to_apply=%region_6.7 | reduce-window | flops 12484608 | bytes 786436 | tf_op jit(solution)/shard_map/reduce-window.2
  9.7 0.4 slice_reduce_fusion
  10.2 0.3 convert_reduce_fusion.1
  10.6 7.0 %gather_fusion.4 = s32[1536]{0:T(1024)S(1)} fusion(s32[6,64]{1,0:T(8,128)S(1)} %sub.34, s32[1536]{0:T(1024)S(1)} %reshape.292), kind=kCustom, calls=%fused_computation.4 | custom fusion | bytes 24576 | tf_op jit(solution)/shard_map/jit(take_along_axis)/gather | solution.py:136
  17.7 6.2 %scatter_custom_fusion = s32[1536]{0:T(1024)S(1)} fusion(s32[1536]{0:T(1024)S(1)} %fusion.26, s32[1536]{0:T(1024)S(1)} %reshape.302, s32[]{:T(128)} %constant.35.clone.1), kind=kCustom, calls=%fused_computation.77 | custom fusion | bytes 6148 | tf_op jit(solution)/shard_map/scatter | solution.py:143
  23.8 0.7 all_to_all.36
  24.5 14.0 %all-to-all-start = ((s32[64,1,24]{2,1,0:T(1,128)}), s32[64,1,24]{2,1,0:T(1,128)S(1)}, u32[]{:S(2)}, u32[]{:S(2)}) async-start(s32[64,1,24]{2,1,0:T(1,128)} %bitcast.5), calls=%async_computation | async-start | bytes 65536 | tf_op jit(solution)/shard_map/all_to_all | solution.py:150
  38.6 6.2 %scatter_custom_fusion.1 = s32[1536]{0:T(1024)S(1)} fusion(s32[1536]{0:T(1024)S(1)} %fusion.26, s32[1536]{0:T(1024)S(1)} %reshape.310, s32[]{:T(128)} %constant.35.clone.1), kind=kCustom, calls=%fused_computation.75 | custom fusion | bytes 6148 | tf_op jit(solution)/shard_map/scatter | solution.py:139
  44.9 0.2 reshape_squeeze.9
  45.1 3.2 %gather_fusion = bf16[1536,64]{1,0:T(8,128)(2,1)S(1)} fusion(bf16[1536,64]{1,0:T(8,128)(2,1)S(1)} %reshape_squeeze.9, s32[2048]{0:T(1024)S(1)} %pad_clamp_fusion.1), kind=kCustom, calls=%fused_computation | custom fusion | bytes 399360 | tf_op jit(solution)/shard_map/gather | solution.py:145
  48.3 0.3 reshape.252
  48.6 0.2 reshape_squeeze.11
  48.8 3.2 %gather_fusion.2 = bf16[1536,64]{1,0:T(8,128)(2,1)S(1)} fusion(bf16[1536,64]{1,0:T(8,128)(2,1)S(1)} %reshape_squeeze.11, s32[2048]{0:T(1024)S(1)} %pad_clamp_fusion.1), kind=kCustom, calls=%fused_computation.2 | custom fusion | bytes 399360 | tf_op jit(solution)/shard_map/gather | solution.py:147
  52.0 0.3 reshape.254
  52.3 0.2 reshape_squeeze.10
  52.5 3.2 %gather_fusion.1 = bf16[1536,64]{1,0:T(8,128)(2,1)S(1)} fusion(bf16[1536,64]{1,0:T(8,128)(2,1)S(1)} %reshape_squeeze.10, s32[2048]{0:T(1024)S(1)} %pad_clamp_fusion.1), kind=kCustom, calls=%fused_computation.1 | custom fusion | bytes 399360 | tf_op jit(solution)/shard_map/gather | solution.py:146
  55.7 0.3 reshape.253
  56.0 0.5 broadcast.252
  56.5 1.0 reduce.10
  57.6 0.9 reshape.334
  58.5 10.3 %all-to-all-start.1 = ((bf16[64,2,2304]{2,1,0:T(2,128)(2,1)}), bf16[64,2,2304]{2,1,0:T(2,128)(2,1)S(1)}, u32[]{:S(2)}, u32[]{:S(2)}) async-start(bf16[64,2,2304]{2,1,0:T(2,128)(2,1)} %reshape.334), calls=%async_computation.1 | async-start | bytes 1179648 | tf_op jit(solution)/shard_map/all_to_all | solution.py:22
  69.0 0.5 broadcast.250
  69.5 0.7 reduce.9
  70.2 0.1 reshape.251
  70.3 16.6 %all-to-all-done.1 = bf16[64,2,2304]{2,1,0:T(2,128)(2,1)S(1)} async-done(((bf16[64,2,2304]{2,1,0:T(2,128)(2,1)}), bf16[64,2,2304]{2,1,0:T(2,128)(2,1)S(1)}, u32[]{:S(2)}, u32[]{:S(2)}) %all-to-all-start.1) | async-done | bytes 589856 | tf_op jit(solution)/shard_map/all_to_all | solution.py:22
  86.9 0.5 reshape.335
  87.5 0.2 reshape.257
  87.8 0.2 reshape.256
  88.0 0.2 reshape.255
  88.3 15.5 %while.11 = (s32[]{:T(128)}, bf16[3,512,64]{1,2,0:T(8,128)(2,1)S(1)}, s32[3]{0:T(128)S(1)}, s32[1536]{0:T(1024)S(1)}, s32[64,24]{1,0:T(8,128)}, /*index=5*/bf16[...) while((s32[]{:T(128)}, ...), condition=%wide.wide.region_14.15_spmd, body=%wide.wide.region_11.14_spmd.sunk | while | flops 211581952 | bytes 10463415 | solution.py:73
  88.3 0.6 dynamic_slice.21
  90.9 0.7 fusion.50
  91.6 0.8 fusion.51
  92.4 1.0 fusion.52
  93.4 0.6 dynamic_slice.21
  96.0 0.7 fusion.50
  96.8 0.8 fusion.51
  97.5 1.0 fusion.52
  98.6 0.6 dynamic_slice.21
  101.2 0.7 fusion.50
  101.9 0.8 fusion.51
  102.7 1.0 fusion.52
  103.8 0.2 copy.59
  104.0 0.3 reshape_reshape_reshape_reshape.3
  104.3 4.2 %all_to_all.53 = bf16[32,2,1,1536]{3,0,2,1:T(8,128)(2,1)S(1)} all-to-all(bf16[32,2,1,1536]{3,0,2,1:T(8,128)(2,1)S(1)} %copy.60), channel_id=1, replica_groups=mesh['tok_0'=4,'tok_1'=8,'tok_2'=2,'head'=8] {'tok_2'}, dimensions={1} | all-to-all | bytes 393216 | tf_op jit(solution)/shard_map/all_to_all | solution.py:42
  108.5 0.9 copy.61
  109.4 6.2 %all-to-all-start.3 = ((bf16[32,2,1,1536]{3,1,2,0:T(2,128)(2,1)}), bf16[32,2,1,1536]{3,1,2,0:T(2,128)(2,1)S(1)}, u32[]{:S(2)}, u32[]{:S(2)}) async-start(bf16[32,2,1,1536]{3,1,2,0:T(2,128)(2,1)} %copy.61), calls=%async_computation.3 | async-start | bytes 393216 | tf_op jit(solution)/shard_map/all_to_all | solution.py:42
  115.6 0.1 copy.62
  115.8 0.1 reshape.258
  116.0 9.4 %all-to-all-done.3 = bf16[32,2,1,1536]{3,1,2,0:T(2,128)(2,1)S(1)} async-done(((bf16[32,2,1,1536]{3,1,2,0:T(2,128)(2,1)}), bf16[32,2,1,1536]{3,1,2,0:T(2,128)(2,1)S(1)}, u32[]{:S(2)}, u32[]{:S(2)}) %all-to-all-start.3) | async-done | bytes 196640 | tf_op jit(solution)/shard_map/all_to_all | solution.py:42
  125.4 0.3 reshape_reshape_reshape.3
  125.7 3.2 %gather_fusion.3 = bf16[1536,64]{1,0:T(8,128)(2,1)S(1)} fusion(bf16[1536,64]{1,0:T(8,128)(2,1)S(1)} %reshape_reshape_reshape.3, s32[2048]{0:T(1024)S(1)} %pad_clamp_fusion), kind=kCustom, calls=%fused_computation.3 | custom fusion | bytes 399360 | tf_op jit(solution)/shard_map/gather | solution.py:163
  128.9 0.3 reshape.259
  129.2 1.1 multiply_convert_fusion
  130.3 16.7 %all_to_all.54 = bf16[8,32,384]{2,1,0:T(8,128)(2,1)S(1)} all-to-all(bf16[8,32,384]{2,1,0:T(8,128)(2,1)S(1)} %bitcast.82), channel_id=1, replica_groups=mesh['tok_0'=4,'tok_1'=8,'tok_2'=2,'head'=8] {'head'}, dimensions={0} | all-to-all | bytes 393216 | tf_op jit(solution)/shard_map/all_to_all | solution.py:167
  147.0 0.1 convert_reduce_fusion.2
  147.1 0.2 fusion.12
  147.4 0.8 fusion.15
  (61 shorter events, 1.2 us)
Async XLA Ops:
  10.6 34.2 %copy-start.1 = (bf16[3,256,384]{2,1,0:T(8,128)(2,1)S(1)}, bf16[3,256,384]{2,1,0:T(8,128)(2,1)}, u32[]{:S(2)}) copy-start(bf16[3,256,384]{2,1,0:T(8,128)(2,1)} %param.12) | copy-start | bytes 1769476
  24.5 34.0 %all-to-all-start = ((s32[64,1,24]{2,1,0:T(1,128)}), s32[64,1,24]{2,1,0:T(1,128)S(1)}, u32[]{:S(2)}, u32[]{:S(2)}) async-start(s32[64,1,24]{2,1,0:T(1,128)} %bitcast.5), calls=%async_computation | async-start | bytes 65536 | tf_op jit(solution)/shard_map/all_to_all | solution.py:150
  58.5 29.2 %copy-start.2 = (s32[64,1,24]{2,1,0:T(1,128)}, s32[64,1,24]{2,1,0:T(1,128)S(1)}, u32[]{:S(2)}) copy-start(s32[64,1,24]{2,1,0:T(1,128)S(1)} %all-to-all-done) | copy-start | bytes 18436
  58.5 28.4 %all-to-all-start.1 = ((bf16[64,2,2304]{2,1,0:T(2,128)(2,1)}), bf16[64,2,2304]{2,1,0:T(2,128)(2,1)S(1)}, u32[]{:S(2)}, u32[]{:S(2)}) async-start(bf16[64,2,2304]{2,1,0:T(2,128)(2,1)} %reshape.334), calls=%async_computation.1 | async-start | bytes 1179648 | tf_op jit(solution)/shard_map/all_to_all | solution.py:22
  104.3 24.9 %copy-start.3 = (bf16[256,384]{1,0:T(8,128)(2,1)S(1)}, bf16[256,384]{1,0:T(8,128)(2,1)}, u32[]{:S(2)}) copy-start(bf16[256,384]{1,0:T(8,128)(2,1)} %param.18) | copy-start | bytes 589828
  104.3 24.9 %copy-start.4 = (bf16[256,384]{1,0:T(8,128)(2,1)S(1)}, bf16[256,384]{1,0:T(8,128)(2,1)}, u32[]{:S(2)}) copy-start(bf16[256,384]{1,0:T(8,128)(2,1)} %param.17) | copy-start | bytes 589828
  104.3 24.9 %copy-start.5 = (bf16[256,384]{1,0:T(8,128)(2,1)S(1)}, bf16[256,384]{1,0:T(8,128)(2,1)}, u32[]{:S(2)}) copy-start(bf16[256,384]{1,0:T(8,128)(2,1)} %param.16) | copy-start | bytes 589828
  104.3 24.9 %copy-start.6 = (bf16[256,384]{1,0:T(8,128)(2,1)S(1)}, bf16[256,384]{1,0:T(8,128)(2,1)}, u32[]{:S(2)}) copy-start(bf16[256,384]{1,0:T(8,128)(2,1)} %param.19) | copy-start | bytes 589828
  109.4 16.0 %all-to-all-start.3 = ((bf16[32,2,1,1536]{3,1,2,0:T(2,128)(2,1)}), bf16[32,2,1,1536]{3,1,2,0:T(2,128)(2,1)S(1)}, u32[]{:S(2)}, u32[]{:S(2)}) async-start(bf16[32,2,1,1536]{3,1,2,0:T(2,128)(2,1)} %copy.61), calls=%async_computation.3 | async-start | bytes 393216 | tf_op jit(solution)/shard_map/all_to_all | solution.py:42
  125.7 21.7 %copy-start.7 = (f32[3072]{0:T(1024)S(1)}, f32[3072]{0:T(1024)}, u32[]{:S(2)}) copy-start(f32[3072]{0:T(1024)} %param.21) | copy-start | bytes 36868
  125.7 21.7 %copy-start.8 = (f32[3072]{0:T(1024)S(1)}, f32[3072]{0:T(1024)}, u32[]{:S(2)}) copy-start(f32[3072]{0:T(1024)} %param.20) | copy-start | bytes 36868
  129.2 19.0 %copy-start = (bf16[256,384]{1,0:T(8,128)(2,1)}, bf16[256,384]{1,0:T(8,128)(2,1)S(1)}, u32[]{:S(2)}) copy-start(bf16[256,384]{1,0:T(8,128)(2,1)S(1)} %reshape.259) | copy-start | bytes 589828
where the time goes:
time: 150 us; the launch traced here: 148 us
  local copies, waits for them, and re-layouts  43.5 us (29%)
  starting transfers between devices  30.6 us (20%)
  waiting for transfers between devices  26 us (17%)
  blocking collectives  20.8 us (14%)
  other arithmetic  14.9 us (10%)
  loops' own time  5.9 us (4%)
  matrix products  5.28 us (4%)
    all_to_all x1, blocking collectives, on_device(): lax.all_to_all(guided, 'head', split_axis=0, concat_axis=1, tiled=True)  16.7 us
    all_to_all x1, waiting for transfers between devices, side_by_side(): lax.all_to_all(both, axis, split_axis=split_dim, concat_axis=concat_dim,...  16.6 us
    all_to_all x1, starting transfers between devices, on_device(): lax.all_to_all(pool_tags.reshape(group_count, pool), TOK, split_axis=0, c...  14 us
    scatter x2, local copies, waits for them, and re-layouts, on_device(): jnp.zeros((group_count * pool,), jnp.int32).at[pool_index.reshape(-1)]  12.4 us
    all_to_all x1, starting transfers between devices, side_by_side(): lax.all_to_all(both, axis, split_axis=split_dim, concat_axis=concat_dim,...  10.3 us
    all_to_all x1, waiting for transfers between devices, exchange_in_order(): lax.all_to_all(tiles, axes[k], split_axis=k, concat_axis=k, tiled=True)  9.43 us
    gather x3, local copies, waits for them, and re-layouts, on_device(): base_offset = jnp.take_along_axis(head_offset, targets, axis=1)  6.99 us
    all_to_all x1, starting transfers between devices, exchange_in_order(): lax.all_to_all(tiles, axes[k], split_axis=k, concat_axis=k, tiled=True)  6.21 us
  transfers between devices with their start and end apart: 3, of which 2 were waited for; matrix products, arithmetic and copies ran while one was open for 15% of the time, Pallas kernels for 0%

commit v1 on v0

v1 whole, which is shorter than its diff:
```python
import jax
import jax.numpy as jnp
from jax import lax
from jax.experimental import pallas as pl
from jax.experimental.pallas import tpu as pltpu
from jax.sharding import Mesh
from jax.sharding import PartitionSpec as P

HEAD_DIM = 64
TOK = ("tok_0", "tok_1", "tok_2")
TOK_HEAD = ("tok_0", "tok_1", "tok_2", "head")
GROUPS = 64
PAIR_ROWS = 8
MASK_OUT = 32768.0
GUIDE_SCALE = 6.0
NORM_EPS = 1e-05
F32, BF16, I32 = jnp.float32, jnp.bfloat16, jnp.int32
NT = (((1,), (1,)), ((), ()))


def iota(shape, dim):
    return lax.broadcasted_iota(I32, shape, dim)


def ones_where(cond):
    return jnp.where(cond, 1.0, 0.0).astype(BF16)


def matmul(a, b):
    return jnp.dot(a, b, preferred_element_type=F32)


def swap_halves(x):
    return pltpu.roll(x, HEAD_DIM, 1)


def pack_kernel(qkv_ref, rank_ref, sizes_ref, owner_ref, send_ref, slot_ref):
    heads, tokens = rank_ref.shape
    clusters = sizes_ref.shape[1]
    pairs = heads // 2
    slots = GROUPS * PAIR_ROWS
    before = ones_where(iota((tokens, tokens), 0) < iota((tokens, tokens), 1))
    upto = ones_where(iota((clusters, clusters), 1) <= iota((clusters, clusters), 0))
    sizes = sizes_ref[...]
    low = (sizes & 255).astype(F32).astype(BF16)
    high = (sizes >> 8).astype(F32).astype(BF16)
    strict = ones_where(iota((clusters, clusters), 1) < iota((clusters, clusters), 0))

    def running(tri):
        return lax.dot_general(tri, low, NT, preferred_element_type=F32) + 256.0 * lax.dot_general(
            tri, high, NT, preferred_element_type=F32
        )

    ends, starts = running(upto), running(strict)
    group_id = iota((GROUPS, 1), 0).astype(F32) * float(PAIR_ROWS)
    left = iota((tokens, 2 * HEAD_DIM), 1) < HEAD_DIM
    values_01 = None
    values_2 = None
    slot_rows = []
    for j in range(pairs):
        places, labels = [], []
        offset = jnp.zeros((GROUPS, 1), F32)
        for half in range(2):
            h = 2 * j + half
            rank = rank_ref[h : h + 1, :].astype(F32)
            member = ones_where((starts[:, h : h + 1] <= rank) & (rank < ends[:, h : h + 1]))
            owned = ones_where(iota((GROUPS, clusters), 0) == owner_ref[h : h + 1, :])
            nth = jnp.sum(owned.astype(F32) * matmul(owned, before), axis=0, keepdims=True)
            label = jnp.where(iota((8, clusters), 0) - 4 * half == nth.astype(I32), 1.0, 0.0)
            rows = matmul(jnp.concatenate([owned.astype(F32), label], axis=0).astype(BF16), member)
            dest = rows[:GROUPS]
            labels.append(rows[GROUPS:])
            earlier = matmul(dest.astype(BF16), before)
            slot = jnp.sum(dest * (group_id + earlier + offset), axis=0, keepdims=True)
            offset = offset + jnp.sum(dest, axis=1, keepdims=True)
            slot_rows.append(slot)
            places.append(ones_where(iota((slots, tokens), 0) == slot.astype(I32)))
        cols = slice(2 * HEAD_DIM * j, 2 * HEAD_DIM * (j + 1))
        q, k, v = (qkv_ref[i, :, cols].astype(F32) for i in range(3))
        qs, ks, vs = swap_halves(q), swap_halves(k), swap_halves(v)
        if j == 1:
            v_even, v_odd = jnp.where(left, 0.0, vs), jnp.where(left, 0.0, v)
        else:
            v_even, v_odd = jnp.where(left, v, 0.0), jnp.where(left, vs, 0.0)
        rhs = jnp.concatenate(
            [
                jnp.concatenate([jnp.where(left, q, ks), v_even], axis=1),
                jnp.concatenate([jnp.where(left, qs, k), v_odd], axis=1),
            ],
            axis=0,
        ).astype(BF16)
        place = jnp.concatenate(places, axis=1)
        sorted_rows = matmul(place, rhs)
        label_rows = jnp.concatenate(labels, axis=1)
        parts = [jnp.zeros((HEAD_DIM + 8 * j, 2 * tokens), F32), label_rows]
        parts.append(jnp.zeros((HEAD_DIM - 8 * (j + 1), 2 * tokens), F32))
        label_lanes = lax.dot_general(
            place, jnp.concatenate(parts, axis=0).astype(BF16), NT, preferred_element_type=F32
        )
        send_ref[:, 8 * j : 8 * (j + 1), :] = (
            sorted_rows[:, : 2 * HEAD_DIM].reshape(GROUPS, 8, 2 * HEAD_DIM).astype(BF16)
        )
        v_rows = sorted_rows[:, 2 * HEAD_DIM :]
        if j == 0:
            values_01, values_2 = v_rows, label_lanes
        elif j == 1:
            values_01, values_2 = values_01 + v_rows, values_2 + label_lanes
        else:
            values_2 = values_2 + v_rows + label_lanes
    send_ref[:, 24:32, :] = values_01.reshape(GROUPS, 8, 2 * HEAD_DIM).astype(BF16)
    send_ref[:, 32:40, :] = values_2.reshape(GROUPS, 8, 2 * HEAD_DIM).astype(BF16)
    slot_rows.append(jnp.zeros((8 - heads, tokens), F32))
    slot_ref[...] = jnp.concatenate(slot_rows, axis=0)


def attend_kernel(recv_ref, back_ref):
    rows = GROUPS * PAIR_ROWS
    wide = 2 * HEAD_DIM

    def block(k):
        return recv_ref[:, 8 * k : 8 * (k + 1), :].reshape(rows, wide)

    lane = iota((rows, wide), 1)
    left = lane < HEAD_DIM
    values_01, values_2 = block(3), block(4)
    marks = values_2.astype(F32)
    outs = []
    for j in range(3):
        qk = block(j).astype(F32)
        own = (lane >= HEAD_DIM + 8 * j) & (lane < HEAD_DIM + 8 * (j + 1))
        a = jnp.where(left, qk, marks).astype(BF16)
        b = jnp.where(
            left, swap_halves(qk), jnp.where(own, MASK_OUT * (marks - 1.0), 0.0)
        ).astype(BF16)
        scores = lax.dot_general(a, b, NT, preferred_element_type=F32)
        largest = jnp.max(scores, axis=1, keepdims=True)
        expo = jnp.exp((scores - largest) * 0.125)
        totals = jnp.sum(expo, axis=1, keepdims=True)
        probs = (expo * (1.0 / totals)).astype(BF16)
        outs.append(matmul(probs, values_2 if j == 2 else values_01))
    back_ref[:, 0:8, :] = jnp.where(left, outs[0], outs[1]).reshape(GROUPS, 8, wide).astype(BF16)
    back_ref[:, 8:16, :] = outs[2].reshape(GROUPS, 8, wide).astype(BF16)


def finish_kernel(
    back_ref, slot_ref, c0_ref, c1_ref, c2_ref, un_ref, zero_ref, one_ref, two_ref, three_ref, guided_ref
):
    tokens = slot_ref.shape[1]
    rows = GROUPS * PAIR_ROWS
    wide = 2 * HEAD_DIM
    slot = jnp.transpose(slot_ref[...]).astype(I32)
    pos = iota((tokens, rows), 1)
    o01 = back_ref[:, 0:8, :].reshape(rows, wide)
    o2 = back_ref[:, 8:16, :].reshape(rows, wide)
    o10 = swap_halves(o01.astype(F32)).astype(BF16)
    o2s = swap_halves(o2.astype(F32)).astype(BF16)
    left = iota((tokens, wide), 1) < HEAD_DIM
    for j, (even, odd) in enumerate(((o01, o10), (o10, o01), (o2, o2s))):
        low = matmul(ones_where(slot[:, 2 * j : 2 * j + 1] == pos), even)
        high = matmul(ones_where(slot[:, 2 * j + 1 : 2 * j + 2] == pos), odd)
        att = jnp.where(left, low, high)
        cols = slice(wide * j, wide * (j + 1))
        zero_ref[:, cols] = att.astype(BF16)
        first = (att - c0_ref[:, cols].astype(F32)) * 0.5
        second = (first - c1_ref[:, cols].astype(F32)) * 0.5
        third = (second - c2_ref[:, cols].astype(F32)) * 0.5
        one_ref[:, cols] = first.astype(BF16)
        two_ref[:, cols] = second.astype(BF16)
        three_ref[:, cols] = third.astype(BF16)
        un = un_ref[:, cols].astype(F32)
        guided_ref[:, cols] = (un + GUIDE_SCALE * (att - un)).astype(BF16)


def norm_kernel(rows_ref, gain_ref, bias_ref, out_ref):
    parts, _, width = rows_ref.shape
    total = parts * width
    blocks = [rows_ref[i].astype(F32) for i in range(parts)]
    mean = sum(jnp.sum(b, axis=1, keepdims=True) for b in blocks) * (1.0 / total)
    blocks = [b - mean for b in blocks]
    var = sum(jnp.sum(b * b, axis=1, keepdims=True) for b in blocks) * (1.0 / total)
    scale = lax.rsqrt(var + NORM_EPS)
    for i, b in enumerate(blocks):
        cols = slice(width * i, width * (i + 1))
        out_ref[:, cols] = (b * scale * gain_ref[:, cols] + bias_ref[:, cols]).astype(BF16)


def call(kernel, outs, *args, **kw):
    vmem = pl.BlockSpec(memory_space=pltpu.VMEM)
    return pl.pallas_call(
        kernel,
        out_shape=[jax.ShapeDtypeStruct(s, t) for s, t in outs],
        in_specs=[vmem] * len(args),
        out_specs=[vmem] * len(outs),
        **kw,
    )(*args)


def pack(qkv, token_rank, cluster_sizes, cluster_owner, **kw):
    tokens = token_rank.shape[1]
    outs = [((GROUPS, 40, 128), BF16), ((8, tokens), F32)]
    return call(pack_kernel, outs, qkv, token_rank, cluster_sizes, cluster_owner, **kw)


def attend(arrived, **kw):
    return call(attend_kernel, [((GROUPS, 16, 128), BF16)], arrived, **kw)[0]


def finish(back, slots, c0, c1, c2, un, **kw):
    return call(finish_kernel, [(c0.shape, BF16)] * 5, back, slots, c0, c1, c2, un, **kw)


def norm(rows, gain, bias, **kw):
    parts, count, width = rows.shape
    outs = [((count, parts * width), BF16)]
    return call(norm_kernel, outs, rows, gain.reshape(1, -1), bias.reshape(1, -1), **kw)[0]


def on_device(qkv, rank, sizes, owner, c0, c1, c2, un, gain, bias):
    send, slots = pack(qkv, rank, sizes, owner)
    arrived = lax.all_to_all(send, TOK, split_axis=0, concat_axis=0, tiled=True)
    back = lax.all_to_all(attend(arrived), TOK, split_axis=0, concat_axis=0, tiled=True)
    zero, one, two, three, guided = finish(back, slots, c0, c1, c2, un)
    blocks = guided.reshape(8, guided.shape[0] // 8, guided.shape[1])
    rows = lax.all_to_all(blocks, "head", split_axis=0, concat_axis=0, tiled=True)
    return norm(rows, gain, bias), zero, one, two, three


def solution(mesh):
    torus = Mesh(mesh.devices.reshape(4, 8, 2, mesh.shape["head"]), TOK_HEAD)
    in_specs = (
        P(None, TOK, "head"),
        P("head", TOK),
        P("head", None),
        P("head", None),
        P(TOK, "head"),
        P(TOK, "head"),
        P(TOK, "head"),
        P(TOK, "head"),
        P(),
        P(),
    )
    out_specs = (P(TOK_HEAD, None), P(TOK, "head"), P(TOK, "head"), P(TOK, "head"), P(TOK, "head"))
    return jax.shard_map(
        on_device, mesh=torus, in_specs=in_specs, out_specs=out_specs, check_vma=False
    )
```

time: 150 us -> 84 us (0.56)
  blocking collectives: 20.8 us -> 70.1 us
  local copies, waits for them, and re-layouts: 43.5 us -> 0 us
  starting transfers between devices: 30.6 us -> 0 us
  waiting for transfers between devices: 26 us -> 0 us
  other arithmetic: 14.9 us -> 0 us
  Pallas kernels: 0 us -> 12.8 us
  loops' own time: 5.9 us -> 0 us
  matrix products: 5.28 us -> 0 us
    all_to_all x2 -> x3, blocking collectives: 20.8 us -> 70.1 us  [the longest x1 33.4 us: on_device(): arrived = lax.all_to_all(send, TOK, split_axis=0, concat_axis=0, tiled=True)]
    all_to_all x3 -> x0, starting transfers between devices: 30.6 us -> none  [the longest x1 14 us: on_device(): lax.all_to_all(pool_tags.reshape(group_count, pool), TOK, split_axis=0, c...]
    all_to_all x3 -> x0, waiting for transfers between devices: 26 us -> none  [the longest x1 16.6 us: side_by_side(): lax.all_to_all(both, axis, split_axis=split_dim, concat_axis=concat_dim,...]
    gather x7 -> x0, local copies, waits for them, and re-layouts: 19.8 us -> none  [the longest x3 6.99 us: on_device(): base_offset = jnp.take_along_axis(head_offset, targets, axis=1)]
    pallas_call x0 -> x4, Pallas kernels: none -> 12.8 us  [call(): pl.pallas_call(kernel, out_shape=[jax.ShapeDtypeStruct(s, t) for s, t in...]
    scatter x2 -> x0, local copies, waits for them, and re-layouts: 12.4 us -> none  [on_device(): jnp.zeros((group_count * pool,), jnp.int32).at[pool_index.reshape(-1)]]
    another operation x1 -> x0, loops' own time: 5.9 us -> none  [attend_pool(): return lax.map(one_block, starts).reshape(total_rows, HEAD_DIM)]
    another operation x5 -> x0, other arithmetic: 5.5 us -> none
  transfers between devices with their start and end apart: 3 -> 0, of which waited for: 2 -> 0; matrix products, arithmetic and copies ran while one was open for 15% -> 0% of each run, Pallas kernels for 0% -> 0%
where the time goes in v1:
time: 84 us; the launch traced here: 83.6 us
  blocking collectives  70.1 us (83%)
  Pallas kernels  12.8 us (15%)
    all_to_all x1, blocking collectives, on_device(): arrived = lax.all_to_all(send, TOK, split_axis=0, concat_axis=0, tiled=True)  33.4 us
    all_to_all x1, blocking collectives, on_device(): lax.all_to_all(attend(arrived), TOK, split_axis=0, concat_axis=0, tiled=T...  18.7 us
    all_to_all x1, blocking collectives, on_device(): lax.all_to_all(blocks, 'head', split_axis=0, concat_axis=0, tiled=True)  18 us
    pallas_call x4, Pallas kernels, call(): pl.pallas_call(kernel, out_shape=[jax.ShapeDtypeStruct(s, t) for s, t in...  12.8 us

profile of v1, /device:TPU:6, one launch (start us, length us, event | category | flops | bytes accessed | tf_op | source)
XLA Modules:
  0.0 83.6 jit_solution(2593897215496876968)
XLA Ops:
  0.6 4.2 %shard_map.137 = (bf16[64,40,128]{2,1,0:T(8,128)(2,1)}, f32[8,256]{1,0:T(8,128)}) custom-call(bf16[3,256,384]{2,1,0:T(8,128)(2,1)} %qkv_ref.1, s32[6,256]{1,0:T(8,128)} %rank_ref.1, s32[6,256]{1,0:T(8,128)} %sizes_ref.1, s32[6,256]{1,0:T(8,128)} %owner_ref.1), custom_call_target="tpu_custom_call" | custom-call | tf_op jit(solution)/shard_map/pallas_call | solution.py:189
  4.8 33.4 %all_to_all.15.recv_ref = bf16[64,40,128]{2,1,0:T(8,128)(2,1)} all-to-all(bf16[64,40,128]{2,1,0:T(8,128)(2,1)} %get-tuple-element.12), channel_id=1, replica_groups=mesh['tok_0'=4,'tok_1'=8,'tok_2'=2,'head'=8] {'tok_0','tok_1','tok_2'}, dimensions={0} | all-to-all | bytes 1310720 | tf_op jit(solution)/shard_map/all_to_all | solution.py:220
  38.2 3.6 %shard_map.138 = bf16[64,16,128]{2,1,0:T(8,128)(2,1)} custom-call(bf16[64,40,128]{2,1,0:T(8,128)(2,1)} %all_to_all.15.recv_ref), custom_call_target="tpu_custom_call" | custom-call | tf_op jit(solution)/shard_map/pallas_call | solution.py:189
  41.9 18.7 %all_to_all.16.back_ref = bf16[64,16,128]{2,1,0:T(8,128)(2,1)} all-to-all(bf16[64,16,128]{2,1,0:T(8,128)(2,1)} %shard_map.138), channel_id=1, replica_groups=mesh['tok_0'=4,'tok_1'=8,'tok_2'=2,'head'=8] {'tok_0','tok_1','tok_2'}, dimensions={0} | all-to-all | bytes 524288 | tf_op jit(solution)/shard_map/all_to_all | solution.py:221
  60.6 3.1 %shard_map.139 = (bf16[256,384]{1,0:T(8,128)(2,1)}, bf16[256,384]{1,0:T(8,128)(2,1)}, bf16[256,384]{1,0:T(8,128)(2,1)}, bf16[256,384]{1,0:T(8,128)(2,1)}, bf16[256,384]{1,0:T(8,128)(2,1)}) custom-call(bf16[64,16,128]{2,1,0:T(8,128)(2,1)} %all_to_all.16.back_ref, f32[8,256]{1,0:T(8,128)} %get-tuple-element.13.slot_ref, bf16[256,384]{1,0:T(8,128)(2,1)} %c0_ref.1, ...), custom_call_target="tpu_custom_call" | custom-call | tf_op jit(solution)/shard_map/pallas_call | solution.py:189
  63.7 18.0 %all_to_all.17.rows_ref = bf16[8,32,384]{2,1,0:T(8,128)(2,1)} all-to-all(bf16[8,32,384]{2,1,0:T(8,128)(2,1)} %bitcast.3), channel_id=1, replica_groups=mesh['tok_0'=4,'tok_1'=8,'tok_2'=2,'head'=8] {'head'}, dimensions={0} | all-to-all | bytes 393216 | tf_op jit(solution)/shard_map/all_to_all | solution.py:224
  81.7 1.9 %shard_map.140 = bf16[32,3072]{1,0:T(8,128)(2,1)} custom-call(bf16[8,32,384]{2,1,0:T(8,128)(2,1)} %all_to_all.17.rows_ref, f32[1,3072]{1,0:T(1,128)} %bitcast.4, f32[1,3072]{1,0:T(1,128)} %bitcast.5), custom_call_target="tpu_custom_call" | custom-call | tf_op jit(solution)/shard_map/pallas_call | solution.py:189

commit v2 on v1

--- a/solution.py
+++ b/solution.py
@@ -188,31 +188,37 @@
     vmem = pl.BlockSpec(memory_space=pltpu.VMEM)
     return pl.pallas_call(
         kernel,
-        out_shape=[jax.ShapeDtypeStruct(s, t) for s, t in outs],
+        out_shape=[pltpu.VMEM(s, t) if stay else jax.ShapeDtypeStruct(s, t) for s, t, stay in outs],
         in_specs=[vmem] * len(args),
         out_specs=[vmem] * len(outs),
         **kw,
     )(*args)
 
 
+def in_vmem(x):
+    return pltpu.with_memory_space_constraint(x, pltpu.VMEM)
+
+
 def pack(qkv, token_rank, cluster_sizes, cluster_owner, **kw):
     tokens = token_rank.shape[1]
-    outs = [((GROUPS, 40, 128), BF16), ((8, tokens), F32)]
+    outs = [((GROUPS, 40, 128), BF16, True), ((8, tokens), F32, True)]
     return call(pack_kernel, outs, qkv, token_rank, cluster_sizes, cluster_owner, **kw)
 
 
 def attend(arrived, **kw):
-    return call(attend_kernel, [((GROUPS, 16, 128), BF16)], arrived, **kw)[0]
+    return call(attend_kernel, [((GROUPS, 16, 128), BF16, True)], in_vmem(arrived), **kw)[0]
 
 
 def finish(back, slots, c0, c1, c2, un, **kw):
-    return call(finish_kernel, [(c0.shape, BF16)] * 5, back, slots, c0, c1, c2, un, **kw)
+    outs = [(c0.shape, BF16, True)] * 5
+    ins = [in_vmem(x) for x in (back, slots, c0, c1, c2, un)]
+    return call(finish_kernel, outs, *ins, **kw)
 
 
 def norm(rows, gain, bias, **kw):
     parts, count, width = rows.shape
-    outs = [((count, parts * width), BF16)]
-    return call(norm_kernel, outs, rows, gain.reshape(1, -1), bias.reshape(1, -1), **kw)[0]
+    outs = [((count, parts * width), BF16, False)]
+    return call(norm_kernel, outs, in_vmem(rows), in_vmem(gain.reshape(1, -1)), in_vmem(bias.reshape(1, -1)), **kw)[0]
 
 
 def on_device(qkv, rank, sizes, owner, c0, c1, c2, un, gain, bias):

time: 84 us -> 78.3 us (0.932)
  blocking collectives: 70.1 us -> 51.7 us
  waiting for transfers between devices: 0 us -> 8.05 us
  starting transfers between devices: 0 us -> 7.1 us
  Pallas kernels: 12.8 us -> 7.74 us
  local copies, waits for them, and re-layouts: 0 us -> 2.73 us
    all_to_all x1 -> x0, blocking collectives: 18 us -> none  [on_device(): lax.all_to_all(blocks, 'head', split_axis=0, concat_axis=0, tiled=True)]
    all_to_all x0 -> x1, waiting for transfers between devices: none -> 8.05 us  [on_device(): lax.all_to_all(blocks, 'head', split_axis=0, concat_axis=0, tiled=True)]
    all_to_all x0 -> x1, starting transfers between devices: none -> 7.1 us  [on_device(): lax.all_to_all(blocks, 'head', split_axis=0, concat_axis=0, tiled=True)]
    pallas_call x4, Pallas kernels: 12.8 us -> 7.74 us  [call(): pl.pallas_call(kernel, out_shape=[pltpu.VMEM(s, t) if stay else jax.Shape...]
    unnamed x0 -> x16, local copies, waits for them, and re-layouts: none -> 2.73 us
  transfers between devices with their start and end apart: 0 -> 1, of which waited for: 0 -> 1; matrix products, arithmetic and copies ran while one was open for 0% -> 3% of each run, Pallas kernels for 0% -> 0%
where the time goes in v2:
time: 78.3 us; the launch traced here: 78 us
  blocking collectives  51.7 us (66%)
  waiting for transfers between devices  8.05 us (10%)
  Pallas kernels  7.74 us (10%)
  starting transfers between devices  7.1 us (9%)
  local copies, waits for them, and re-layouts  2.73 us (3%)
    all_to_all x1, blocking collectives, on_device(): arrived = lax.all_to_all(send, TOK, split_axis=0, concat_axis=0, tiled=True)  33.1 us
    all_to_all x1, blocking collectives, on_device(): lax.all_to_all(attend(arrived), TOK, split_axis=0, concat_axis=0, tiled=T...  18.5 us
    all_to_all x1, waiting for transfers between devices, on_device(): lax.all_to_all(blocks, 'head', split_axis=0, concat_axis=0, tiled=True)  8.05 us
    pallas_call x4, Pallas kernels, call(): pl.pallas_call(kernel, out_shape=[pltpu.VMEM(s, t) if stay else jax.Shape...  7.74 us
    all_to_all x1, starting transfers between devices, on_device(): lax.all_to_all(blocks, 'head', split_axis=0, concat_axis=0, tiled=True)  7.1 us
    unnamed x16, local copies, waits for them, and re-layouts  2.73 us
  transfers between devices with their start and end apart: 1, of which 1 were waited for; matrix products, arithmetic and copies ran while one was open for 3% of the time, Pallas kernels for 0%

profile of v2, /device:TPU:6, one launch (start us, length us, event | category | flops | bytes accessed | tf_op | source)
XLA Modules:
  0.0 78.0 jit_solution(2560324315137269719)
XLA Ops:
  0.6 3.3 %shard_map.137 = (bf16[64,40,128]{2,1,0:T(8,128)(2,1)S(1)}, f32[8,256]{1,0:T(8,128)S(1)}) custom-call(bf16[3,256,384]{2,1,0:T(8,128)(2,1)} %qkv_ref.1, s32[6,256]{1,0:T(8,128)} %rank_ref.1, s32[6,256]{1,0:T(8,128)} %sizes_ref.1, s32[6,256]{1,0:T(8,128)} %owner_ref.1), custom_call_target="tpu_custom_call" | custom-call | tf_op jit(solution)/shard_map/pallas_call | solution.py:189
  4.0 33.1 %all_to_all.15.recv_ref = bf16[64,40,128]{2,1,0:T(8,128)(2,1)S(1)} all-to-all(bf16[64,40,128]{2,1,0:T(8,128)(2,1)S(1)} %get-tuple-element.12), channel_id=1, replica_groups=mesh['tok_0'=4,'tok_1'=8,'tok_2'=2,'head'=8] {'tok_0','tok_1','tok_2'}, dimensions={0} | all-to-all | bytes 1310720 | tf_op jit(solution)/shard_map/all_to_all | solution.py:226
  37.1 0.0 copy-start.2
  37.1 0.0 copy-start.3
  37.1 1.8 %shard_map.138 = bf16[64,16,128]{2,1,0:T(8,128)(2,1)S(1)} custom-call(bf16[64,40,128]{2,1,0:T(8,128)(2,1)S(1)} %all_to_all.15.recv_ref), custom_call_target="tpu_custom_call" | custom-call | tf_op jit(solution)/shard_map/pallas_call | solution.py:189
  38.9 0.0 copy-start
  38.9 0.0 copy-start.1
  39.0 18.5 %all_to_all.16.back_ref = bf16[64,16,128]{2,1,0:T(8,128)(2,1)S(1)} all-to-all(bf16[64,16,128]{2,1,0:T(8,128)(2,1)S(1)} %shard_map.138), channel_id=1, replica_groups=mesh['tok_0'=4,'tok_1'=8,'tok_2'=2,'head'=8] {'tok_0','tok_1','tok_2'}, dimensions={0} | all-to-all | bytes 524288 | tf_op jit(solution)/shard_map/all_to_all | solution.py:227
  57.5 0.0 copy-done.2
  57.5 0.0 copy-done.3
  57.5 0.0 copy-done
  57.5 0.0 copy-done.1
  57.5 1.6 %shard_map.139 = (bf16[256,384]{1,0:T(8,128)(2,1)S(1)}, bf16[256,384]{1,0:T(8,128)(2,1)S(1)}, bf16[256,384]{1,0:T(8,128)(2,1)S(1)}, bf16[256,384]{1,0:T(8,128)(2,1)S(1)}, bf16[256,384]{1,0:T(8,128)(2,1)}) custom-call(bf16[64,16,128]{2,1,0:T(8,128)(2,1)S(1)} %all_to_all.16.back_ref, f32[8,256]{1,0:T(8,128)S(1)} %get-tuple-element.13.slot_ref, ...), custom_call_target="tpu_custom_call" | custom-call | tf_op jit(solution)/shard_map/pallas_call | solution.py:189
  59.1 7.1 %all-to-all-start.2 = ((bf16[8,32,384]{2,1,0:T(8,128)(2,1)}), bf16[8,32,384]{2,1,0:T(8,128)(2,1)S(1)}, u32[]{:S(2)}, u32[]{:S(2)}) async-start(bf16[8,32,384]{2,1,0:T(8,128)(2,1)} %bitcast), calls=%async_computation.2 | async-start | bytes 393216 | tf_op jit(solution)/shard_map/all_to_all | solution.py:230
  66.2 0.7 copy.15
  66.9 0.7 copy.16
  67.6 0.7 copy.17
  68.2 0.0 copy-start.4
  68.2 0.0 copy-start.5
  68.2 0.7 copy.18
  68.9 8.1 %all-to-all-done.2.rows_ref = bf16[8,32,384]{2,1,0:T(8,128)(2,1)S(1)} async-done(((bf16[8,32,384]{2,1,0:T(8,128)(2,1)}), bf16[8,32,384]{2,1,0:T(8,128)(2,1)S(1)}, u32[]{:S(2)}, u32[]{:S(2)}) %all-to-all-start.2) | async-done | bytes 196640 | tf_op jit(solution)/shard_map/all_to_all | solution.py:230
  77.0 0.0 copy-done.4
  77.0 0.0 copy-done.5
  77.0 1.0 %shard_map.140 = bf16[32,3072]{1,0:T(8,128)(2,1)} custom-call(bf16[8,32,384]{2,1,0:T(8,128)(2,1)S(1)} %all-to-all-done.2.rows_ref, f32[1,3072]{1,0:T(1,128)S(1)} %bitcast.3, f32[1,3072]{1,0:T(1,128)S(1)} %bitcast.4), custom_call_target="tpu_custom_call" | custom-call | tf_op jit(solution)/shard_map/pallas_call | solution.py:189
Async XLA Ops:
  37.1 20.4 %copy-start.2 = (bf16[256,384]{1,0:T(8,128)(2,1)S(1)}, bf16[256,384]{1,0:T(8,128)(2,1)}, u32[]{:S(2)}) copy-start(bf16[256,384]{1,0:T(8,128)(2,1)} %c2_ref.1) | copy-start | bytes 589828
  37.1 20.4 %copy-start.3 = (bf16[256,384]{1,0:T(8,128)(2,1)S(1)}, bf16[256,384]{1,0:T(8,128)(2,1)}, u32[]{:S(2)}) copy-start(bf16[256,384]{1,0:T(8,128)(2,1)} %un_ref.1) | copy-start | bytes 589828
  38.9 18.6 %copy-start = (bf16[256,384]{1,0:T(8,128)(2,1)S(1)}, bf16[256,384]{1,0:T(8,128)(2,1)}, u32[]{:S(2)}) copy-start(bf16[256,384]{1,0:T(8,128)(2,1)} %c0_ref.1) | copy-start | bytes 589828
  38.9 18.6 %copy-start.1 = (bf16[256,384]{1,0:T(8,128)(2,1)S(1)}, bf16[256,384]{1,0:T(8,128)(2,1)}, u32[]{:S(2)}) copy-start(bf16[256,384]{1,0:T(8,128)(2,1)} %c1_ref.1) | copy-start | bytes 589828
  59.1 17.9 %all-to-all-start.2 = ((bf16[8,32,384]{2,1,0:T(8,128)(2,1)}), bf16[8,32,384]{2,1,0:T(8,128)(2,1)S(1)}, u32[]{:S(2)}, u32[]{:S(2)}) async-start(bf16[8,32,384]{2,1,0:T(8,128)(2,1)} %bitcast), calls=%async_computation.2 | async-start | bytes 393216 | tf_op jit(solution)/shard_map/all_to_all | solution.py:230
  68.2 8.7 %copy-start.4 = (f32[3072]{0:T(1024)S(1)}, f32[3072]{0:T(1024)}, u32[]{:S(2)}) copy-start(f32[3072]{0:T(1024)} %param.18) | copy-start | bytes 36868
  68.2 8.7 %copy-start.5 = (f32[3072]{0:T(1024)S(1)}, f32[3072]{0:T(1024)}, u32[]{:S(2)}) copy-start(f32[3072]{0:T(1024)} %param.19) | copy-start | bytes 36868

commit v3 on v2

v3 whole, which is shorter than its diff:
```python
import math

import jax
import jax.numpy as jnp
from jax import lax
from jax.experimental import pallas as pl
from jax.experimental.pallas import tpu as pltpu
from jax.sharding import Mesh
from jax.sharding import PartitionSpec as P

HEAD_DIM = 64
TOK = ("tok_0", "tok_1", "tok_2")
TOK_HEAD = ("tok_0", "tok_1", "tok_2", "head")
GROUPS = 64
PAIR_ROWS = 8
MASK_OUT = 32768.0
GUIDE_SCALE = 6.0
NORM_EPS = 1e-05
EXPONENT = math.log2(math.e) / math.sqrt(HEAD_DIM)
F32, BF16, I32 = jnp.float32, jnp.bfloat16, jnp.int32
NT = (((1,), (1,)), ((), ()))


def iota(shape, dim):
    return lax.broadcasted_iota(I32, shape, dim)


def ones_where(cond):
    return jnp.where(cond, 1.0, 0.0).astype(BF16)


def one_hot(cond):
    return jnp.where(cond, jnp.ones(cond.shape, BF16), jnp.zeros(cond.shape, BF16))


def matmul(a, b):
    return jnp.dot(a, b, preferred_element_type=F32)


def swap_halves(x):
    return pltpu.roll(x, HEAD_DIM, 1)


def pack_kernel(
    parity_ref, qkv_hbm, rank_ref, sizes_ref, owner_ref, send_ref, row_ref, qkv_ref, sem
):
    fetch = pltpu.make_async_copy(qkv_hbm, qkv_ref, sem)
    fetch.start()
    heads, tokens = rank_ref.shape
    clusters = sizes_ref.shape[1]
    pairs = heads // 2
    slots = GROUPS * PAIR_ROWS
    before = ones_where(iota((tokens, tokens), 0) < iota((tokens, tokens), 1))
    strict = ones_where(iota((clusters, clusters), 1) < iota((clusters, clusters), 0))
    sizes = sizes_ref[...]
    low = (sizes & 255).astype(F32).astype(BF16)
    high = (sizes >> 8).astype(F32).astype(BF16)
    starts = lax.dot_general(strict, low, NT, preferred_element_type=F32)
    starts = starts + 256.0 * lax.dot_general(strict, high, NT, preferred_element_type=F32)
    owned = [
        jnp.where(iota((GROUPS, clusters), 0) == owner_ref[h : h + 1, :], 1.0, 0.0)
        for h in range(heads)
    ]
    counts = matmul(jnp.concatenate(owned, axis=0).astype(BF16), before)
    first = iota((GROUPS + 8, clusters), 1) == 0
    dests, labels = [], []
    for h in range(heads):
        nth = jnp.sum(owned[h] * counts[GROUPS * h : GROUPS * (h + 1)], axis=0, keepdims=True)
        label = jnp.where(iota((8, clusters), 0) - 4 * (h % 2) == nth.astype(I32), 1.0, 0.0)
        table = jnp.concatenate([owned[h], label], axis=0)
        step = table - jnp.where(first, 0.0, pltpu.roll(table, 1, 1))
        reached = ones_where(starts[:, h : h + 1] <= rank_ref[h : h + 1, :].astype(F32))
        rows = matmul(step.astype(BF16), reached)
        dests.append(rows[:GROUPS])
        labels.append(rows[GROUPS:])
    earlier = matmul(jnp.concatenate(dests, axis=0).astype(BF16), before)
    group_id = iota((GROUPS, 1), 0).astype(F32) * float(PAIR_ROWS)
    slots_iota = iota((slots, tokens), 0).astype(jnp.int16)
    slot_rows, places = [], []
    for h in range(heads):
        offset = group_id
        if h % 2:
            offset = offset + jnp.sum(dests[h - 1], axis=1, keepdims=True)
        ahead = earlier[GROUPS * h : GROUPS * (h + 1)] + offset
        slot = jnp.sum(dests[h] * ahead, axis=0, keepdims=True)
        slot_rows.append(slot)
        places.append(one_hot(slots_iota == slot.astype(I32).astype(jnp.int16)))
    slot = jnp.concatenate(slot_rows, axis=0).astype(I32)
    group, place = slot >> 3, slot & 7
    mixed_row = 12 * group + 4 * parity_ref[0] + place
    last_row = 12 * group + 8 - 8 * parity_ref[0] + (place & 3)
    back_row = jnp.where(iota(slot.shape, 0) < 4, mixed_row, last_row)
    row_ref[...] = jnp.concatenate([back_row, place[4:6] >> 2], axis=0).astype(F32)
    left = iota((tokens, 2 * HEAD_DIM), 1) < HEAD_DIM
    lane = iota((tokens, 2 * HEAD_DIM), 1)
    marks = []
    for half in range(2):
        zeros = jnp.zeros((HEAD_DIM, tokens), F32)
        rest = jnp.zeros((HEAD_DIM - 8 * pairs, tokens), F32)
        marks.append(jnp.transpose(jnp.concatenate([zeros, *labels[half::2], rest], axis=0)))
    fetch.wait()
    values = []
    for j in range(pairs):
        cols = slice(2 * HEAD_DIM * j, 2 * HEAD_DIM * (j + 1))
        own = (lane >= HEAD_DIM + 8 * j) & (lane < HEAD_DIM + 8 * (j + 1))
        even, odd = (jnp.where(own, m, 0.0) for m in marks)
        q, k, v = (qkv_ref[i, :, cols].astype(F32) for i in range(3))
        qs, ks, vs = swap_halves(q), swap_halves(k), swap_halves(v)
        even = jnp.concatenate([jnp.where(left, q, ks), jnp.where(left, v, even)], axis=1)
        odd = jnp.concatenate([jnp.where(left, qs, k), jnp.where(left, vs, odd)], axis=1)
        place = jnp.concatenate(places[2 * j : 2 * j + 2], axis=1)
        sorted_rows = matmul(place, jnp.concatenate([even, odd], axis=0).astype(BF16))
        send_ref[:, 8 * j : 8 * (j + 1), :] = (
            sorted_rows[:, : 2 * HEAD_DIM].reshape(GROUPS, 8, 2 * HEAD_DIM).astype(BF16)
        )
        values.append(sorted_rows[:, 2 * HEAD_DIM :])
    left = iota((slots, 2 * HEAD_DIM), 1) < HEAD_DIM
    first = jnp.where(left, values[0], swap_halves(values[1]))
    second = jnp.where(left, values[2], values[0] + values[1] + values[2])
    send_ref[:, 24:32, :] = first.reshape(GROUPS, 8, 2 * HEAD_DIM).astype(BF16)
    send_ref[:, 32:40, :] = second.reshape(GROUPS, 8, 2 * HEAD_DIM).astype(BF16)


def attend_kernel(recv_ref, back_ref):
    rows = GROUPS * PAIR_ROWS
    wide = 2 * HEAD_DIM

    def block(k):
        return recv_ref[:, 8 * k : 8 * (k + 1), :].reshape(rows, wide)

    lane = iota((rows, wide), 1)
    left = lane < HEAD_DIM
    values_01 = block(3)
    marks = block(4).astype(F32)
    values_2 = jnp.where(left, marks, swap_halves(marks)).astype(BF16)
    outs = []
    for j in range(3):
        qk = block(j).astype(F32)
        own = (lane >= HEAD_DIM + 8 * j) & (lane < HEAD_DIM + 8 * (j + 1))
        a = jnp.where(left, qk, marks).astype(BF16)
        b = jnp.where(
            left, swap_halves(qk), jnp.where(own, MASK_OUT * (marks - 1.0), 0.0)
        ).astype(BF16)
        scores = lax.dot_general(a, b, NT, preferred_element_type=F32)
        largest = jnp.max(scores, axis=1, keepdims=True)
        expo = jnp.exp2((scores - largest) * EXPONENT)
        totals = jnp.sum(expo, axis=1, keepdims=True)
        probs = (expo * (1.0 / totals)).astype(BF16)
        outs.append(matmul(probs, values_2 if j == 2 else values_01))
    shape = (GROUPS // 2, 2, 8, wide)
    mixed = jnp.where(left, outs[0], outs[1]).reshape(shape).astype(BF16)
    back_ref[:, 0:8, :] = mixed[:, 0]
    back_ref[:, 16:24, :] = mixed[:, 1]
    last = outs[2].reshape(GROUPS, 8, wide)
    turned = pltpu.roll(last, 4, 1).reshape(shape)
    last = last.reshape(shape)
    near = iota((GROUPS // 2, 8, wide), 2) < HEAD_DIM
    upper = iota((GROUPS // 2, 8, wide), 1) < 4
    back_ref[:, 8:16, :] = jnp.where(
        upper,
        jnp.where(near, last[:, 0], turned[:, 0]),
        jnp.where(near, turned[:, 1], last[:, 1]),
    ).astype(BF16)


def finish_kernel(back_ref, row_ref, un_ref, att_ref, guided_ref):
    tokens = row_ref.shape[1]
    rows = back_ref.shape[0]
    wide = 2 * HEAD_DIM
    table = jnp.transpose(row_ref[...])
    row = table.astype(I32).astype(jnp.int16)
    pos = iota((tokens, rows), 1).astype(jnp.int16)
    kept = back_ref[...]
    turned = swap_halves(kept.astype(F32)).astype(BF16)
    left = iota((tokens, wide), 1) < HEAD_DIM
    for j in range(3):
        picks = [one_hot(row[:, h : h + 1] == pos) for h in (2 * j, 2 * j + 1)]
        if j < 2:
            low = matmul(picks[0], turned if j else kept)
            high = matmul(picks[1], kept if j else turned)
        else:
            low, high = matmul(picks[0], kept), matmul(picks[1], kept)
            low = jnp.where(table[:, 6:7] > 0.5, swap_halves(low), low)
            high = jnp.where(table[:, 7:8] > 0.5, high, swap_halves(high))
        att = jnp.where(left, low, high)
        cols = slice(wide * j, wide * (j + 1))
        att_ref[:, cols] = att.astype(BF16)
        un = un_ref[:, cols].astype(F32)
        guided_ref[:, cols] = (un + GUIDE_SCALE * (att - un)).astype(BF16)


def last_kernel(rows_ref, gain_ref, bias_ref, att_ref, c0_ref, c1_ref, c2_ref, *refs):
    outs, buffers, sem = refs[:5], refs[5:9], refs[9]
    copies = []

    def send(ref, out):
        copies.append(pltpu.make_async_copy(ref, out, sem.at[len(copies)]))
        copies[-1].start()

    send(att_ref, outs[1])
    parts, _, width = rows_ref.shape
    total = parts * width
    blocks = [rows_ref[i].astype(F32) for i in range(parts)]
    mean = sum(jnp.sum(b, axis=1, keepdims=True) for b in blocks) * (1.0 / total)
    blocks = [b - mean for b in blocks]
    var = sum(jnp.sum(b * b, axis=1, keepdims=True) for b in blocks) * (1.0 / total)
    scale = lax.rsqrt(var + NORM_EPS)
    for i, b in enumerate(blocks):
        cols = slice(width * i, width * (i + 1))
        buffers[0][:, cols] = (b * scale * gain_ref[:, cols] + bias_ref[:, cols]).astype(BF16)
    send(buffers[0], outs[0])
    first = (att_ref[...].astype(F32) - c0_ref[...].astype(F32)) * 0.5
    buffers[1][...] = first.astype(BF16)
    send(buffers[1], outs[2])
    second = (first - c1_ref[...].astype(F32)) * 0.5
    buffers[2][...] = second.astype(BF16)
    send(buffers[2], outs[3])
    buffers[3][...] = ((second - c2_ref[...].astype(F32)) * 0.5).astype(BF16)
    send(buffers[3], outs[4])
    for copy in copies:
        copy.wait()


VMEM = pl.BlockSpec(memory_space=pltpu.VMEM)
HBM = pl.BlockSpec(memory_space=pl.ANY)
SMEM = pl.BlockSpec(memory_space=pltpu.SMEM)


def in_vmem(x):
    return pltpu.with_memory_space_constraint(x, pltpu.VMEM)


def call(kernel, outs, in_specs, *args, **kw):
    return pl.pallas_call(
        kernel, out_shape=outs, in_specs=in_specs, out_specs=[VMEM] * len(outs), **kw
    )(*args)


def pack(parity, qkv, token_rank, cluster_sizes, cluster_owner, **kw):
    tokens = token_rank.shape[1]
    outs = [pltpu.VMEM((GROUPS, 40, 128), BF16), pltpu.VMEM((8, tokens), F32)]
    scratch = [pltpu.VMEM(qkv.shape, BF16), pltpu.SemaphoreType.DMA]
    args = (parity, qkv, token_rank, cluster_sizes, cluster_owner)
    specs = [SMEM, HBM, VMEM, VMEM, VMEM]
    return call(pack_kernel, outs, specs, *args, scratch_shapes=scratch, **kw)


def attend(arrived, **kw):
    outs = [pltpu.VMEM((GROUPS // 2, 24, 128), BF16)]
    back = call(attend_kernel, outs, [VMEM], in_vmem(arrived), **kw)[0]
    return back.reshape(GROUPS, 3, 4, 128)


def finish(back, table, un, **kw):
    outs = [pltpu.VMEM(un.shape, BF16)] * 2
    args = [in_vmem(x) for x in (back.reshape(GROUPS * 12, 128), table, un)]
    return call(finish_kernel, outs, [VMEM] * 3, *args, **kw)


def last(rows, gain, bias, att, c0, c1, c2, **kw):
    parts, count, width = rows.shape
    shapes = [(count, parts * width)] + [att.shape] * 4
    args = [in_vmem(x) for x in (rows, gain.reshape(1, -1), bias.reshape(1, -1), att, c0, c1, c2)]
    return pl.pallas_call(
        last_kernel,
        out_shape=[jax.ShapeDtypeStruct(s, BF16) for s in shapes],
        in_specs=[VMEM] * 7,
        out_specs=[HBM] * 5,
        scratch_shapes=[pltpu.VMEM(s, BF16) for s in shapes[:1] + shapes[2:]]
        + [pltpu.SemaphoreType.DMA((5,))],
        **kw,
    )(*args)


def on_device(qkv, rank, sizes, owner, c0, c1, c2, un, gain, bias):
    parity = lax.axis_index("tok_2").reshape(1)
    send, table = pack(parity, qkv, rank, sizes, owner)
    arrived = lax.all_to_all(send, TOK, split_axis=0, concat_axis=0, tiled=True)
    back = lax.all_to_all(attend(arrived), TOK, split_axis=0, concat_axis=0, tiled=True)
    att, guided = finish(back, table, un)
    blocks = guided.reshape(8, guided.shape[0] // 8, guided.shape[1])
    rows = lax.all_to_all(blocks, "head", split_axis=0, concat_axis=0, tiled=True)
    return tuple(last(rows, gain, bias, att, c0, c1, c2))


def solution(mesh):
    torus = Mesh(mesh.devices.reshape(4, 8, 2, mesh.shape["head"]), TOK_HEAD)
    in_specs = (
        P(None, TOK, "head"),
        P("head", TOK),
        P("head", None),
        P("head", None),
        P(TOK, "head"),
        P(TOK, "head"),
        P(TOK, "head"),
        P(TOK, "head"),
        P(),
        P(),
    )
    out_specs = (P(TOK_HEAD, None), P(TOK, "head"), P(TOK, "head"), P(TOK, "head"), P(TOK, "head"))
    return jax.shard_map(
        on_device, mesh=torus, in_specs=in_specs, out_specs=out_specs, check_vma=False
    )
```

time: 78.3 us -> 75.8 us (0.968)
  blocking collectives: 51.7 us -> 68.1 us
  waiting for transfers between devices: 8.05 us -> 0 us
  starting transfers between devices: 7.1 us -> 0 us
  local copies, waits for them, and re-layouts: 2.73 us -> 0.03 us
  Pallas kernels: 7.74 us -> 6.66 us
    all_to_all x0 -> x1, blocking collectives: none -> 17.8 us  [on_device(): lax.all_to_all(blocks, 'head', split_axis=0, concat_axis=0, tiled=True)]
    all_to_all x1 -> x0, waiting for transfers between devices: 8.05 us -> none  [on_device(): lax.all_to_all(blocks, 'head', split_axis=0, concat_axis=0, tiled=True)]
    all_to_all x1 -> x0, starting transfers between devices: 7.1 us -> none  [on_device(): lax.all_to_all(blocks, 'head', split_axis=0, concat_axis=0, tiled=True)]
    unnamed x16 -> x12, local copies, waits for them, and re-layouts: 2.73 us -> 0.03 us
    all_to_all x1, blocking collectives: 18.5 us -> 17.2 us  [on_device(): lax.all_to_all(attend(arrived), TOK, split_axis=0, concat_axis=0, tiled=T...]
    pallas_call x4, Pallas kernels: 7.74 us -> 6.66 us  [the longest x3 5.4 us: call(): pl.pallas_call(kernel, out_shape=outs, in_specs=in_specs, out_specs=[VMEM...]
  transfers between devices with their start and end apart: 1 -> 0, of which waited for: 1 -> 0; matrix products, arithmetic and copies ran while one was open for 3% -> 0% of each run, Pallas kernels for 0% -> 0%
where the time goes in v3:
time: 75.8 us; the launch traced here: 75.5 us
  blocking collectives  68.1 us (90%)
  Pallas kernels  6.66 us (9%)
    all_to_all x1, blocking collectives, on_device(): arrived = lax.all_to_all(send, TOK, split_axis=0, concat_axis=0, tiled=True)  33.1 us
    all_to_all x1, blocking collectives, on_device(): lax.all_to_all(blocks, 'head', split_axis=0, concat_axis=0, tiled=True)  17.8 us
    all_to_all x1, blocking collectives, on_device(): lax.all_to_all(attend(arrived), TOK, split_axis=0, concat_axis=0, tiled=T...  17.2 us
    pallas_call x3, Pallas kernels, call(): pl.pallas_call(kernel, out_shape=outs, in_specs=in_specs, out_specs=[VMEM...  5.4 us

profile of v3, /device:TPU:6, one launch (start us, length us, event | category | flops | bytes accessed | tf_op | source)
XLA Modules:
  0.0 75.5 jit_solution(15906337967322080148)
XLA Ops:
  0.6 2.6 %shard_map.137 = (bf16[64,40,128]{2,1,0:T(8,128)(2,1)S(1)}, f32[8,256]{1,0:T(8,128)S(1)}) custom-call(s32[1]{0:T(128)} %bitcast.parity_ref, bf16[3,256,384]{2,1,0:T(8,128)(2,1)} %qkv_hbm.1, s32[6,256]{1,0:T(8,128)} %rank_ref.1, s32[6,256]{1,0:T(8,128)} %sizes_ref.1, s32[6,256]{1,0:T(8,128)} %owner_ref.1), custom_call_target="tpu_custom_call" | custom-call | tf_op jit(solution)/shard_map/pallas_call | solution.py:234
  3.2 33.1 %all_to_all.15.recv_ref = bf16[64,40,128]{2,1,0:T(8,128)(2,1)S(1)} all-to-all(bf16[64,40,128]{2,1,0:T(8,128)(2,1)S(1)} %get-tuple-element.9), channel_id=1, replica_groups=mesh['tok_0'=4,'tok_1'=8,'tok_2'=2,'head'=8] {'tok_0','tok_1','tok_2'}, dimensions={0} | all-to-all | bytes 1310720 | tf_op jit(solution)/shard_map/all_to_all | solution.py:278
  36.3 1.8 %shard_map.138 = bf16[32,24,128]{2,1,0:T(8,128)(2,1)S(1)} custom-call(bf16[64,40,128]{2,1,0:T(8,128)(2,1)S(1)} %all_to_all.15.recv_ref), custom_call_target="tpu_custom_call" | custom-call | tf_op jit(solution)/shard_map/pallas_call | solution.py:234
  38.1 0.0 copy-start
  38.1 17.2 %all_to_all.16 = bf16[64,3,4,128]{3,2,1,0:T(4,128)(2,1)S(1)} all-to-all(bf16[64,3,4,128]{3,2,1,0:T(4,128)(2,1)S(1)} %bitcast.7), channel_id=1, replica_groups=mesh['tok_0'=4,'tok_1'=8,'tok_2'=2,'head'=8] {'tok_0','tok_1','tok_2'}, dimensions={0} | all-to-all | bytes 393216 | tf_op jit(solution)/shard_map/all_to_all | solution.py:279
  55.3 0.0 copy-done
  55.3 0.0 copy-start.3
  55.3 0.0 copy-start.4
  55.3 0.0 copy-start.5
  55.3 1.1 %shard_map.139 = (bf16[256,384]{1,0:T(8,128)(2,1)S(1)}, bf16[256,384]{1,0:T(8,128)(2,1)S(1)}) custom-call(bf16[768,128]{1,0:T(8,128)(2,1)S(1)} %bitcast.6, f32[8,256]{1,0:T(8,128)S(1)} %get-tuple-element.10.row_ref, bf16[256,384]{1,0:T(8,128)(2,1)S(1)} %copy-done), custom_call_target="tpu_custom_call" | custom-call | tf_op jit(solution)/shard_map/pallas_call | solution.py:234
  56.4 0.0 copy-start.1
  56.4 0.0 copy-start.2
  56.4 17.8 %all_to_all.17.rows_ref = bf16[8,32,384]{2,1,0:T(8,128)(2,1)S(1)} all-to-all(bf16[8,32,384]{2,1,0:T(8,128)(2,1)S(1)} %bitcast.8), channel_id=1, replica_groups=mesh['tok_0'=4,'tok_1'=8,'tok_2'=2,'head'=8] {'head'}, dimensions={0} | all-to-all | bytes 393216 | tf_op jit(solution)/shard_map/all_to_all | solution.py:282
  74.2 0.0 copy-done.3
  74.2 0.0 copy-done.4
  74.2 0.0 copy-done.5
  74.2 0.0 copy-done.1
  74.2 0.0 copy-done.2
  74.2 1.3 %shard_map.140 = (bf16[32,3072]{1,0:T(8,128)(2,1)}, bf16[256,384]{1,0:T(8,128)(2,1)}, bf16[256,384]{1,0:T(8,128)(2,1)}, bf16[256,384]{1,0:T(8,128)(2,1)}, bf16[256,384]{1,0:T(8,128)(2,1)}) custom-call(bf16[8,32,384]{2,1,0:T(8,128)(2,1)S(1)} %all_to_all.17.rows_ref, f32[1,3072]{1,0:T(1,128)S(1)} %bitcast.9, f32[1,3072]{1,0:T(1,128)S(1)} %bitcast.10, ...), custom_call_target="tpu_custom_call" | custom-call | tf_op jit(solution)/shard_map/pallas_call | solution.py:264
Async XLA Ops:
  38.1 17.2 %copy-start = (bf16[256,384]{1,0:T(8,128)(2,1)S(1)}, bf16[256,384]{1,0:T(8,128)(2,1)}, u32[]{:S(2)}) copy-start(bf16[256,384]{1,0:T(8,128)(2,1)} %un_ref.1) | copy-start | bytes 589828
  55.3 18.9 %copy-start.3 = (bf16[256,384]{1,0:T(8,128)(2,1)S(1)}, bf16[256,384]{1,0:T(8,128)(2,1)}, u32[]{:S(2)}) copy-start(bf16[256,384]{1,0:T(8,128)(2,1)} %c2_ref.1) | copy-start | bytes 589828
  55.3 18.9 %copy-start.4 = (f32[3072]{0:T(1024)S(1)}, f32[3072]{0:T(1024)}, u32[]{:S(2)}) copy-start(f32[3072]{0:T(1024)} %param.18) | copy-start | bytes 36868
  55.3 18.9 %copy-start.5 = (f32[3072]{0:T(1024)S(1)}, f32[3072]{0:T(1024)}, u32[]{:S(2)}) copy-start(f32[3072]{0:T(1024)} %param.19) | copy-start | bytes 36868
  56.4 17.8 %copy-start.1 = (bf16[256,384]{1,0:T(8,128)(2,1)S(1)}, bf16[256,384]{1,0:T(8,128)(2,1)}, u32[]{:S(2)}) copy-start(bf16[256,384]{1,0:T(8,128)(2,1)} %c0_ref.1) | copy-start | bytes 589828
  56.4 17.8 %copy-start.2 = (bf16[256,384]{1,0:T(8,128)(2,1)S(1)}, bf16[256,384]{1,0:T(8,128)(2,1)}, u32[]{:S(2)}) copy-start(bf16[256,384]{1,0:T(8,128)(2,1)} %c1_ref.1) | copy-start | bytes 589828

commit v4 on v3

--- a/solution.py
+++ b/solution.py
@@ -5,12 +5,10 @@
 from jax import lax
 from jax.experimental import pallas as pl
 from jax.experimental.pallas import tpu as pltpu
-from jax.sharding import Mesh
 from jax.sharding import PartitionSpec as P
 
 HEAD_DIM = 64
-TOK = ("tok_0", "tok_1", "tok_2")
-TOK_HEAD = ("tok_0", "tok_1", "tok_2", "head")
+OUT_FIRST, BACK_FIRST, HEAD_FIRST = 45, 45, 5
 GROUPS = 64
 PAIR_ROWS = 8
 MASK_OUT = 32768.0
@@ -86,7 +84,7 @@
         slot_rows.append(slot)
         places.append(one_hot(slots_iota == slot.astype(I32).astype(jnp.int16)))
     slot = jnp.concatenate(slot_rows, axis=0).astype(I32)
-    group, place = slot >> 3, slot & 7
+    group, place = ((slot >> 3) + (OUT_FIRST - BACK_FIRST)) & (GROUPS - 1), slot & 7
     mixed_row = 12 * group + 4 * parity_ref[0] + place
     last_row = 12 * group + 8 - 8 * parity_ref[0] + (place & 3)
     back_row = jnp.where(iota(slot.shape, 0) < 4, mixed_row, last_row)
@@ -121,6 +119,16 @@
     send_ref[:, 32:40, :] = second.reshape(GROUPS, 8, 2 * HEAD_DIM).astype(BF16)
 
 
+def put(back_ref, row, value):
+    pairs = value.shape[0]
+    shift = (OUT_FIRST - BACK_FIRST) // 2 % pairs
+    if shift:
+        back_ref[shift:, row : row + 8, :] = value[: pairs - shift]
+        back_ref[:shift, row : row + 8, :] = value[pairs - shift :]
+    else:
+        back_ref[:, row : row + 8, :] = value
+
+
 def attend_kernel(recv_ref, back_ref):
     rows = GROUPS * PAIR_ROWS
     wide = 2 * HEAD_DIM
@@ -149,18 +157,19 @@
         outs.append(matmul(probs, values_2 if j == 2 else values_01))
     shape = (GROUPS // 2, 2, 8, wide)
     mixed = jnp.where(left, outs[0], outs[1]).reshape(shape).astype(BF16)
-    back_ref[:, 0:8, :] = mixed[:, 0]
-    back_ref[:, 16:24, :] = mixed[:, 1]
+    put(back_ref, 0, mixed[:, 0])
+    put(back_ref, 16, mixed[:, 1])
     last = outs[2].reshape(GROUPS, 8, wide)
     turned = pltpu.roll(last, 4, 1).reshape(shape)
     last = last.reshape(shape)
     near = iota((GROUPS // 2, 8, wide), 2) < HEAD_DIM
     upper = iota((GROUPS // 2, 8, wide), 1) < 4
-    back_ref[:, 8:16, :] = jnp.where(
+    last = jnp.where(
         upper,
         jnp.where(near, last[:, 0], turned[:, 0]),
         jnp.where(near, turned[:, 1], last[:, 1]),
-    ).astype(BF16)
+    )
+    put(back_ref, 8, last.astype(BF16))
 
 
 def finish_kernel(back_ref, row_ref, un_ref, att_ref, guided_ref):
@@ -186,7 +195,11 @@
         cols = slice(wide * j, wide * (j + 1))
         att_ref[:, cols] = att.astype(BF16)
         un = un_ref[:, cols].astype(F32)
-        guided_ref[:, cols] = (un + GUIDE_SCALE * (att - un)).astype(BF16)
+        guided = (un + GUIDE_SCALE * (att - un)).astype(BF16)
+        parts, count, _ = guided_ref.shape
+        for i in range(parts):
+            at = (i + HEAD_FIRST) % parts * count
+            guided_ref[i, :, cols] = guided[at : at + count]
 
 
 def last_kernel(rows_ref, gain_ref, bias_ref, att_ref, c0_ref, c1_ref, c2_ref, *refs):
@@ -206,7 +219,8 @@
     var = sum(jnp.sum(b * b, axis=1, keepdims=True) for b in blocks) * (1.0 / total)
     scale = lax.rsqrt(var + NORM_EPS)
     for i, b in enumerate(blocks):
-        cols = slice(width * i, width * (i + 1))
+        at = (i + HEAD_FIRST) % parts
+        cols = slice(width * at, width * (at + 1))
         buffers[0][:, cols] = (b * scale * gain_ref[:, cols] + bias_ref[:, cols]).astype(BF16)
     send(buffers[0], outs[0])
     first = (att_ref[...].astype(F32) - c0_ref[...].astype(F32)) * 0.5
@@ -252,7 +266,7 @@
 
 
 def finish(back, table, un, **kw):
-    outs = [pltpu.VMEM(un.shape, BF16)] * 2
+    outs = [pltpu.VMEM(un.shape, BF16), pltpu.VMEM((8, un.shape[0] // 8, un.shape[1]), BF16)]
     args = [in_vmem(x) for x in (back.reshape(GROUPS * 12, 128), table, un)]
     return call(finish_kernel, outs, [VMEM] * 3, *args, **kw)
 
@@ -272,32 +286,27 @@
     )(*args)
 
 
+def exchange(x, axis, first):
+    size = lax.axis_size(axis)
+    order = [[(first + i) % size for i in range(size)]]
+    return lax.all_to_all(x, axis, 0, 0, axis_index_groups=order, tiled=True)
+
+
 def on_device(qkv, rank, sizes, owner, c0, c1, c2, un, gain, bias):
-    parity = lax.axis_index("tok_2").reshape(1)
+    parity = ((lax.axis_index("tok") + BACK_FIRST) % 2).reshape(1)
     send, table = pack(parity, qkv, rank, sizes, owner)
-    arrived = lax.all_to_all(send, TOK, split_axis=0, concat_axis=0, tiled=True)
-    back = lax.all_to_all(attend(arrived), TOK, split_axis=0, concat_axis=0, tiled=True)
+    arrived = exchange(send, "tok", OUT_FIRST)
+    back = exchange(attend(arrived), "tok", BACK_FIRST)
     att, guided = finish(back, table, un)
-    blocks = guided.reshape(8, guided.shape[0] // 8, guided.shape[1])
-    rows = lax.all_to_all(blocks, "head", split_axis=0, concat_axis=0, tiled=True)
+    rows = exchange(guided, "head", HEAD_FIRST)
     return tuple(last(rows, gain, bias, att, c0, c1, c2))
 
 
 def solution(mesh):
-    torus = Mesh(mesh.devices.reshape(4, 8, 2, mesh.shape["head"]), TOK_HEAD)
-    in_specs = (
-        P(None, TOK, "head"),
-        P("head", TOK),
-        P("head", None),
-        P("head", None),
-        P(TOK, "head"),
-        P(TOK, "head"),
-        P(TOK, "head"),
-        P(TOK, "head"),
-        P(),
-        P(),
+    cached = P("tok", "head")
+    in_specs = (P(None, "tok", "head"), P("head", "tok"), P("head", None), P("head", None))
+    in_specs = in_specs + (cached,) * 4 + (P(), P())
+    out_specs = (P(("tok", "head"), None),) + (cached,) * 4
+    return jax.shard_map(
+        on_device, mesh=mesh, in_specs=in_specs, out_specs=out_specs, check_vma=False
     )
-    out_specs = (P(TOK_HEAD, None), P(TOK, "head"), P(TOK, "head"), P(TOK, "head"), P(TOK, "head"))
-    return jax.shard_map(
-        on_device, mesh=torus, in_specs=in_specs, out_specs=out_specs, check_vma=False
-    )

time: 75.8 us -> 69 us (0.910)
  blocking collectives: 68.1 us -> 61.2 us
    all_to_all x3, blocking collectives: 68.1 us -> 61.2 us  [exchange(): return lax.all_to_all(x, axis, 0, 0, axis_index_groups=order, tiled=True)]
where the time goes in v4:
time: 69 us; the launch traced here: 68.6 us
  blocking collectives  61.2 us (89%)
  Pallas kernels  6.65 us (10%)
  between operations  0.72 us (1%)
    all_to_all x3, blocking collectives, exchange(): return lax.all_to_all(x, axis, 0, 0, axis_index_groups=order, tiled=True)  61.2 us
    pallas_call x3, Pallas kernels, call(): pl.pallas_call(kernel, out_shape=outs, in_specs=in_specs, out_specs=[VMEM...  5.4 us

profile of v4, /device:TPU:6, one launch (start us, length us, event | category | flops | bytes accessed | tf_op | source)
XLA Modules:
  0.0 68.6 jit_solution(711571450367486047)
XLA Ops:
  0.6 2.6 %shard_map.137 = (bf16[64,40,128]{2,1,0:T(8,128)(2,1)S(1)}, f32[8,256]{1,0:T(8,128)S(1)}) custom-call(s32[1]{0:T(128)} %bitcast.parity_ref, bf16[3,256,384]{2,1,0:T(8,128)(2,1)} %qkv_hbm.1, s32[6,256]{1,0:T(8,128)} %rank_ref.1, s32[6,256]{1,0:T(8,128)} %sizes_ref.1, s32[6,256]{1,0:T(8,128)} %owner_ref.1), custom_call_target="tpu_custom_call" | custom-call | tf_op jit(solution)/shard_map/pallas_call | solution.py:248
  3.2 31.9 %all_to_all.15.recv_ref = bf16[64,40,128]{2,1,0:T(8,128)(2,1)S(1)} all-to-all(bf16[64,40,128]{2,1,0:T(8,128)(2,1)S(1)} %get-tuple-element.9), channel_id=1, replica_groups={{360,368,376,384,392,400,408,416,424,432,440,448,456,464,472,480,488,49..., dimensions={0} | all-to-all | bytes 1310720 | tf_op jit(solution)/shard_map/all_to_all | solution.py:292
  35.1 1.8 %shard_map.138 = bf16[32,24,128]{2,1,0:T(8,128)(2,1)S(1)} custom-call(bf16[64,40,128]{2,1,0:T(8,128)(2,1)S(1)} %all_to_all.15.recv_ref), custom_call_target="tpu_custom_call" | custom-call | tf_op jit(solution)/shard_map/pallas_call | solution.py:248
  36.9 0.0 copy-start
  36.9 16.0 %all_to_all.16 = bf16[64,3,4,128]{3,2,1,0:T(4,128)(2,1)S(1)} all-to-all(bf16[64,3,4,128]{3,2,1,0:T(4,128)(2,1)S(1)} %bitcast.6), channel_id=1, replica_groups={{360,368,376,384,392,400,408,416,424,432,440,448,456,464,472,480,488,49..., dimensions={0} | all-to-all | bytes 393216 | tf_op jit(solution)/shard_map/all_to_all | solution.py:292
  52.9 0.0 copy-done
  52.9 0.0 copy-start.3
  52.9 0.0 copy-start.4
  52.9 0.0 copy-start.5
  52.9 1.1 %shard_map.139 = (bf16[256,384]{1,0:T(8,128)(2,1)S(1)}, bf16[8,32,384]{2,1,0:T(8,128)(2,1)S(1)}) custom-call(bf16[768,128]{1,0:T(8,128)(2,1)S(1)} %bitcast.5, f32[8,256]{1,0:T(8,128)S(1)} %get-tuple-element.10.row_ref, bf16[256,384]{1,0:T(8,128)(2,1)S(1)} %copy-done), custom_call_target="tpu_custom_call" | custom-call | tf_op jit(solution)/shard_map/pallas_call | solution.py:248
  54.0 0.0 copy-start.1
  54.0 0.0 copy-start.2
  54.0 13.4 %all_to_all.17.rows_ref = bf16[8,32,384]{2,1,0:T(8,128)(2,1)S(1)} all-to-all(bf16[8,32,384]{2,1,0:T(8,128)(2,1)S(1)} %get-tuple-element.11), channel_id=1, replica_groups={{5,6,7,0,1,2,3,4},{13,14,15,8,9,10,11,12},{21,22,23,16,17,18,19,20},{29..., dimensions={0} | all-to-all | bytes 393216 | tf_op jit(solution)/shard_map/all_to_all | solution.py:292
  67.4 0.0 copy-done.3
  67.4 0.0 copy-done.4
  67.4 0.0 copy-done.5
  67.4 0.0 copy-done.1
  67.4 0.0 copy-done.2
  67.4 1.3 %shard_map.140 = (bf16[32,3072]{1,0:T(8,128)(2,1)}, bf16[256,384]{1,0:T(8,128)(2,1)}, bf16[256,384]{1,0:T(8,128)(2,1)}, bf16[256,384]{1,0:T(8,128)(2,1)}, bf16[256,384]{1,0:T(8,128)(2,1)}) custom-call(bf16[8,32,384]{2,1,0:T(8,128)(2,1)S(1)} %all_to_all.17.rows_ref, f32[1,3072]{1,0:T(1,128)S(1)} %bitcast.7, f32[1,3072]{1,0:T(1,128)S(1)} %bitcast.8, ...), custom_call_target="tpu_custom_call" | custom-call | tf_op jit(solution)/shard_map/pallas_call | solution.py:278
Async XLA Ops:
  36.9 16.0 %copy-start = (bf16[256,384]{1,0:T(8,128)(2,1)S(1)}, bf16[256,384]{1,0:T(8,128)(2,1)}, u32[]{:S(2)}) copy-start(bf16[256,384]{1,0:T(8,128)(2,1)} %un_ref.1) | copy-start | bytes 589828
  52.9 14.5 %copy-start.3 = (bf16[256,384]{1,0:T(8,128)(2,1)S(1)}, bf16[256,384]{1,0:T(8,128)(2,1)}, u32[]{:S(2)}) copy-start(bf16[256,384]{1,0:T(8,128)(2,1)} %c2_ref.1) | copy-start | bytes 589828
  52.9 14.5 %copy-start.4 = (f32[3072]{0:T(1024)S(1)}, f32[3072]{0:T(1024)}, u32[]{:S(2)}) copy-start(f32[3072]{0:T(1024)} %param.18) | copy-start | bytes 36868
  52.9 14.5 %copy-start.5 = (f32[3072]{0:T(1024)S(1)}, f32[3072]{0:T(1024)}, u32[]{:S(2)}) copy-start(f32[3072]{0:T(1024)} %param.19) | copy-start | bytes 36868
  54.0 13.4 %copy-start.1 = (bf16[256,384]{1,0:T(8,128)(2,1)S(1)}, bf16[256,384]{1,0:T(8,128)(2,1)}, u32[]{:S(2)}) copy-start(bf16[256,384]{1,0:T(8,128)(2,1)} %c0_ref.1) | copy-start | bytes 589828
  54.0 13.4 %copy-start.2 = (bf16[256,384]{1,0:T(8,128)(2,1)S(1)}, bf16[256,384]{1,0:T(8,128)(2,1)}, u32[]{:S(2)}) copy-start(bf16[256,384]{1,0:T(8,128)(2,1)} %c1_ref.1) | copy-start | bytes 589828

commit v5 on v4

--- a/solution.py
+++ b/solution.py
@@ -8,7 +8,10 @@
 from jax.sharding import PartitionSpec as P
 
 HEAD_DIM = 64
-OUT_FIRST, BACK_FIRST, HEAD_FIRST = 45, 45, 5
+TOK_ORDER = [
+    (16 * (x % 4)) + 2 * (z % 8) + core for core in (1, 0) for z in range(6, 14) for x in range(2, 6)
+]
+HEAD_ORDER = [5, 1, 6, 2, 7, 3, 0, 4]
 GROUPS = 64
 PAIR_ROWS = 8
 MASK_OUT = 32768.0
@@ -40,16 +43,36 @@
 
 
 def pack_kernel(
-    parity_ref, qkv_hbm, rank_ref, sizes_ref, owner_ref, send_ref, row_ref, qkv_ref, sem
+    parity_ref,
+    qkv_hbm,
+    rank_hbm,
+    sizes_hbm,
+    owner_hbm,
+    send_ref,
+    row_ref,
+    sizes_ref,
+    owner_ref,
+    rank_ref,
+    qkv_ref,
+    sem,
 ):
-    fetch = pltpu.make_async_copy(qkv_hbm, qkv_ref, sem)
-    fetch.start()
+    sources = (sizes_hbm, owner_hbm, rank_hbm, qkv_hbm)
+    targets = (sizes_ref, owner_ref, rank_ref, qkv_ref)
+    fetches = [
+        pltpu.make_async_copy(src, dst, sem.at[i])
+        for i, (src, dst) in enumerate(zip(sources, targets))
+    ]
+    for fetch in fetches:
+        fetch.start()
     heads, tokens = rank_ref.shape
     clusters = sizes_ref.shape[1]
     pairs = heads // 2
     slots = GROUPS * PAIR_ROWS
     before = ones_where(iota((tokens, tokens), 0) < iota((tokens, tokens), 1))
     strict = ones_where(iota((clusters, clusters), 1) < iota((clusters, clusters), 0))
+    slots_iota = iota((slots, tokens), 0).astype(jnp.int16)
+    for fetch in fetches[:3]:
+        fetch.wait()
     sizes = sizes_ref[...]
     low = (sizes & 255).astype(F32).astype(BF16)
     high = (sizes >> 8).astype(F32).astype(BF16)
@@ -73,7 +96,6 @@
         labels.append(rows[GROUPS:])
     earlier = matmul(jnp.concatenate(dests, axis=0).astype(BF16), before)
     group_id = iota((GROUPS, 1), 0).astype(F32) * float(PAIR_ROWS)
-    slots_iota = iota((slots, tokens), 0).astype(jnp.int16)
     slot_rows, places = [], []
     for h in range(heads):
         offset = group_id
@@ -84,7 +106,7 @@
         slot_rows.append(slot)
         places.append(one_hot(slots_iota == slot.astype(I32).astype(jnp.int16)))
     slot = jnp.concatenate(slot_rows, axis=0).astype(I32)
-    group, place = ((slot >> 3) + (OUT_FIRST - BACK_FIRST)) & (GROUPS - 1), slot & 7
+    group, place = slot >> 3, slot & 7
     mixed_row = 12 * group + 4 * parity_ref[0] + place
     last_row = 12 * group + 8 - 8 * parity_ref[0] + (place & 3)
     back_row = jnp.where(iota(slot.shape, 0) < 4, mixed_row, last_row)
@@ -96,7 +118,7 @@
         zeros = jnp.zeros((HEAD_DIM, tokens), F32)
         rest = jnp.zeros((HEAD_DIM - 8 * pairs, tokens), F32)
         marks.append(jnp.transpose(jnp.concatenate([zeros, *labels[half::2], rest], axis=0)))
-    fetch.wait()
+    fetches[3].wait()
     values = []
     for j in range(pairs):
         cols = slice(2 * HEAD_DIM * j, 2 * HEAD_DIM * (j + 1))
@@ -119,16 +141,6 @@
     send_ref[:, 32:40, :] = second.reshape(GROUPS, 8, 2 * HEAD_DIM).astype(BF16)
 
 
-def put(back_ref, row, value):
-    pairs = value.shape[0]
-    shift = (OUT_FIRST - BACK_FIRST) // 2 % pairs
-    if shift:
-        back_ref[shift:, row : row + 8, :] = value[: pairs - shift]
-        back_ref[:shift, row : row + 8, :] = value[pairs - shift :]
-    else:
-        back_ref[:, row : row + 8, :] = value
-
-
 def attend_kernel(recv_ref, back_ref):
     rows = GROUPS * PAIR_ROWS
     wide = 2 * HEAD_DIM
@@ -141,24 +153,33 @@
     values_01 = block(3)
     marks = block(4).astype(F32)
     values_2 = jnp.where(left, marks, swap_halves(marks)).astype(BF16)
-    outs = []
-    for j in range(3):
+
+    def operands(j):
         qk = block(j).astype(F32)
         own = (lane >= HEAD_DIM + 8 * j) & (lane < HEAD_DIM + 8 * (j + 1))
         a = jnp.where(left, qk, marks).astype(BF16)
         b = jnp.where(
             left, swap_halves(qk), jnp.where(own, MASK_OUT * (marks - 1.0), 0.0)
         ).astype(BF16)
-        scores = lax.dot_general(a, b, NT, preferred_element_type=F32)
+        return a, b
+
+    def score(ab):
+        return lax.dot_general(ab[0], ab[1], NT, preferred_element_type=F32)
+
+    def softmax(scores):
         largest = jnp.max(scores, axis=1, keepdims=True)
         expo = jnp.exp2((scores - largest) * EXPONENT)
         totals = jnp.sum(expo, axis=1, keepdims=True)
-        probs = (expo * (1.0 / totals)).astype(BF16)
-        outs.append(matmul(probs, values_2 if j == 2 else values_01))
+        return (expo * (1.0 / totals)).astype(BF16)
+
+    ab = [operands(j) for j in range(3)]
+    scores = [score(x) for x in ab]
+    probs = [softmax(x) for x in scores]
+    outs = [matmul(p, values_2 if j == 2 else values_01) for j, p in enumerate(probs)]
     shape = (GROUPS // 2, 2, 8, wide)
     mixed = jnp.where(left, outs[0], outs[1]).reshape(shape).astype(BF16)
-    put(back_ref, 0, mixed[:, 0])
-    put(back_ref, 16, mixed[:, 1])
+    back_ref[:, 0:8, :] = mixed[:, 0]
+    back_ref[:, 16:24, :] = mixed[:, 1]
     last = outs[2].reshape(GROUPS, 8, wide)
     turned = pltpu.roll(last, 4, 1).reshape(shape)
     last = last.reshape(shape)
@@ -169,7 +190,7 @@
         jnp.where(near, last[:, 0], turned[:, 0]),
         jnp.where(near, turned[:, 1], last[:, 1]),
     )
-    put(back_ref, 8, last.astype(BF16))
+    back_ref[:, 8:16, :] = last.astype(BF16)
 
 
 def finish_kernel(back_ref, row_ref, un_ref, att_ref, guided_ref):
@@ -180,15 +201,14 @@
     row = table.astype(I32).astype(jnp.int16)
     pos = iota((tokens, rows), 1).astype(jnp.int16)
     kept = back_ref[...]
-    turned = swap_halves(kept.astype(F32)).astype(BF16)
     left = iota((tokens, wide), 1) < HEAD_DIM
     for j in range(3):
-        picks = [one_hot(row[:, h : h + 1] == pos) for h in (2 * j, 2 * j + 1)]
-        if j < 2:
-            low = matmul(picks[0], turned if j else kept)
-            high = matmul(picks[1], kept if j else turned)
+        low, high = (matmul(one_hot(row[:, h : h + 1] == pos), kept) for h in (2 * j, 2 * j + 1))
+        if j == 0:
+            high = swap_halves(high)
+        elif j == 1:
+            low = swap_halves(low)
         else:
-            low, high = matmul(picks[0], kept), matmul(picks[1], kept)
             low = jnp.where(table[:, 6:7] > 0.5, swap_halves(low), low)
             high = jnp.where(table[:, 7:8] > 0.5, high, swap_halves(high))
         att = jnp.where(left, low, high)
@@ -198,7 +218,7 @@
         guided = (un + GUIDE_SCALE * (att - un)).astype(BF16)
         parts, count, _ = guided_ref.shape
         for i in range(parts):
-            at = (i + HEAD_FIRST) % parts * count
+            at = HEAD_ORDER[i] * count
             guided_ref[i, :, cols] = guided[at : at + count]
 
 
@@ -219,18 +239,19 @@
     var = sum(jnp.sum(b * b, axis=1, keepdims=True) for b in blocks) * (1.0 / total)
     scale = lax.rsqrt(var + NORM_EPS)
     for i, b in enumerate(blocks):
-        at = (i + HEAD_FIRST) % parts
-        cols = slice(width * at, width * (at + 1))
+        cols = slice(width * HEAD_ORDER[i], width * (HEAD_ORDER[i] + 1))
         buffers[0][:, cols] = (b * scale * gain_ref[:, cols] + bias_ref[:, cols]).astype(BF16)
     send(buffers[0], outs[0])
-    first = (att_ref[...].astype(F32) - c0_ref[...].astype(F32)) * 0.5
-    buffers[1][...] = first.astype(BF16)
-    send(buffers[1], outs[2])
-    second = (first - c1_ref[...].astype(F32)) * 0.5
-    buffers[2][...] = second.astype(BF16)
-    send(buffers[2], outs[3])
-    buffers[3][...] = ((second - c2_ref[...].astype(F32)) * 0.5).astype(BF16)
-    send(buffers[3], outs[4])
+    chunk = att_ref.shape[0] // 4
+    for start in range(0, att_ref.shape[0], chunk):
+        rows = slice(start, start + chunk)
+        first = (att_ref[rows].astype(F32) - c0_ref[rows].astype(F32)) * 0.5
+        second = (first - c1_ref[rows].astype(F32)) * 0.5
+        third = (second - c2_ref[rows].astype(F32)) * 0.5
+        for i, term in enumerate((first, second, third)):
+            buffers[1 + i][rows] = term.astype(BF16)
+    for i in range(3):
+        send(buffers[1 + i], outs[2 + i])
     for copy in copies:
         copy.wait()
 
@@ -253,9 +274,10 @@
 def pack(parity, qkv, token_rank, cluster_sizes, cluster_owner, **kw):
     tokens = token_rank.shape[1]
     outs = [pltpu.VMEM((GROUPS, 40, 128), BF16), pltpu.VMEM((8, tokens), F32)]
-    scratch = [pltpu.VMEM(qkv.shape, BF16), pltpu.SemaphoreType.DMA]
+    scratch = [pltpu.VMEM(x.shape, x.dtype) for x in (cluster_sizes, cluster_owner, token_rank, qkv)]
+    scratch.append(pltpu.SemaphoreType.DMA((4,)))
     args = (parity, qkv, token_rank, cluster_sizes, cluster_owner)
-    specs = [SMEM, HBM, VMEM, VMEM, VMEM]
+    specs = [SMEM, HBM, HBM, HBM, HBM]
     return call(pack_kernel, outs, specs, *args, scratch_shapes=scratch, **kw)
 
 
@@ -286,19 +308,17 @@
     )(*args)
 
 
-def exchange(x, axis, first):
-    size = lax.axis_size(axis)
-    order = [[(first + i) % size for i in range(size)]]
-    return lax.all_to_all(x, axis, 0, 0, axis_index_groups=order, tiled=True)
+def exchange(x, axis, order):
+    return lax.all_to_all(x, axis, 0, 0, axis_index_groups=[order], tiled=True)
 
 
 def on_device(qkv, rank, sizes, owner, c0, c1, c2, un, gain, bias):
-    parity = ((lax.axis_index("tok") + BACK_FIRST) % 2).reshape(1)
+    parity = ((lax.axis_index("tok") >> 4) & 1).reshape(1)
     send, table = pack(parity, qkv, rank, sizes, owner)
-    arrived = exchange(send, "tok", OUT_FIRST)
-    back = exchange(attend(arrived), "tok", BACK_FIRST)
+    arrived = exchange(send, "tok", TOK_ORDER)
+    back = exchange(attend(arrived), "tok", TOK_ORDER)
     att, guided = finish(back, table, un)
-    rows = exchange(guided, "head", HEAD_FIRST)
+    rows = exchange(guided, "head", HEAD_ORDER)
     return tuple(last(rows, gain, bias, att, c0, c1, c2))
 
 

time: 69 us -> 68 us (0.986)
  no operation moved by 1% of the time
where the time goes in v5:
time: 68 us; the launch traced here: 67.7 us
  blocking collectives  60.8 us (89%)
  Pallas kernels  6.21 us (9%)
  between operations  0.71 us (1%)
    all_to_all x3, blocking collectives, exchange(): return lax.all_to_all(x, axis, 0, 0, axis_index_groups=[order], tiled=True)  60.8 us
    pallas_call x3, Pallas kernels, call(): pl.pallas_call(kernel, out_shape=outs, in_specs=in_specs, out_specs=[VMEM...  5 us

profile of v5, /device:TPU:6, one launch (start us, length us, event | category | flops | bytes accessed | tf_op | source)
XLA Modules:
  0.0 67.7 jit_solution(18053872998489670666)
XLA Ops:
  0.6 2.4 %shard_map.137 = (bf16[64,40,128]{2,1,0:T(8,128)(2,1)S(1)}, f32[8,256]{1,0:T(8,128)S(1)}) custom-call(s32[1]{0:T(128)} %bitcast.parity_ref, bf16[3,256,384]{2,1,0:T(8,128)(2,1)} %qkv_hbm.1, s32[6,256]{1,0:T(8,128)} %rank_hbm.1, s32[6,256]{1,0:T(8,128)} %sizes_hbm.1, s32[6,256]{1,0:T(8,128)} %owner_hbm.1), custom_call_target="tpu_custom_call" | custom-call | tf_op jit(solution)/shard_map/pallas_call | solution.py:269
  3.0 31.0 %all_to_all.15.recv_ref = bf16[64,40,128]{2,1,0:T(8,128)(2,1)S(1)} all-to-all(bf16[64,40,128]{2,1,0:T(8,128)(2,1)S(1)} %get-tuple-element.9), channel_id=1, replica_groups={{360,488,104,232,376,504,120,248,264,392,8,136,280,408,24,152,296,424,4..., dimensions={0} | all-to-all | bytes 1310720 | tf_op jit(solution)/shard_map/all_to_all | solution.py:312
  34.0 1.6 %shard_map.138 = bf16[32,24,128]{2,1,0:T(8,128)(2,1)S(1)} custom-call(bf16[64,40,128]{2,1,0:T(8,128)(2,1)S(1)} %all_to_all.15.recv_ref), custom_call_target="tpu_custom_call" | custom-call | tf_op jit(solution)/shard_map/pallas_call | solution.py:269
  35.6 0.0 copy-start
  35.6 16.1 %all_to_all.16 = bf16[64,3,4,128]{3,2,1,0:T(4,128)(2,1)S(1)} all-to-all(bf16[64,3,4,128]{3,2,1,0:T(4,128)(2,1)S(1)} %bitcast.6), channel_id=1, replica_groups={{360,488,104,232,376,504,120,248,264,392,8,136,280,408,24,152,296,424,4..., dimensions={0} | all-to-all | bytes 393216 | tf_op jit(solution)/shard_map/all_to_all | solution.py:312
  51.7 0.0 copy-done
  51.7 0.0 copy-start.3
  51.7 0.0 copy-start.4
  51.7 0.0 copy-start.5
  51.7 1.0 %shard_map.139 = (bf16[256,384]{1,0:T(8,128)(2,1)S(1)}, bf16[8,32,384]{2,1,0:T(8,128)(2,1)S(1)}) custom-call(bf16[768,128]{1,0:T(8,128)(2,1)S(1)} %bitcast.5, f32[8,256]{1,0:T(8,128)S(1)} %get-tuple-element.10.row_ref, bf16[256,384]{1,0:T(8,128)(2,1)S(1)} %copy-done), custom_call_target="tpu_custom_call" | custom-call | tf_op jit(solution)/shard_map/pallas_call | solution.py:269
  52.8 0.0 copy-start.1
  52.8 0.0 copy-start.2
  52.8 13.7 %all_to_all.17.rows_ref = bf16[8,32,384]{2,1,0:T(8,128)(2,1)S(1)} all-to-all(bf16[8,32,384]{2,1,0:T(8,128)(2,1)S(1)} %get-tuple-element.11), channel_id=1, replica_groups={{5,1,6,2,7,3,0,4},{13,9,14,10,15,11,8,12},{21,17,22,18,23,19,16,20},{29..., dimensions={0} | all-to-all | bytes 393216 | tf_op jit(solution)/shard_map/all_to_all | solution.py:312
  66.5 0.0 copy-done.3
  66.5 0.0 copy-done.4
  66.5 0.0 copy-done.5
  66.5 0.0 copy-done.1
  66.5 0.0 copy-done.2
  66.5 1.2 %shard_map.140 = (bf16[32,3072]{1,0:T(8,128)(2,1)}, bf16[256,384]{1,0:T(8,128)(2,1)}, bf16[256,384]{1,0:T(8,128)(2,1)}, bf16[256,384]{1,0:T(8,128)(2,1)}, bf16[256,384]{1,0:T(8,128)(2,1)}) custom-call(bf16[8,32,384]{2,1,0:T(8,128)(2,1)S(1)} %all_to_all.17.rows_ref, f32[1,3072]{1,0:T(1,128)S(1)} %bitcast.7, f32[1,3072]{1,0:T(1,128)S(1)} %bitcast.8, ...), custom_call_target="tpu_custom_call" | custom-call | tf_op jit(solution)/shard_map/pallas_call | solution.py:300
Async XLA Ops:
  35.6 16.2 %copy-start = (bf16[256,384]{1,0:T(8,128)(2,1)S(1)}, bf16[256,384]{1,0:T(8,128)(2,1)}, u32[]{:S(2)}) copy-start(bf16[256,384]{1,0:T(8,128)(2,1)} %un_ref.1) | copy-start | bytes 589828
  51.7 14.8 %copy-start.3 = (bf16[256,384]{1,0:T(8,128)(2,1)S(1)}, bf16[256,384]{1,0:T(8,128)(2,1)}, u32[]{:S(2)}) copy-start(bf16[256,384]{1,0:T(8,128)(2,1)} %c2_ref.1) | copy-start | bytes 589828
  51.7 14.8 %copy-start.4 = (f32[3072]{0:T(1024)S(1)}, f32[3072]{0:T(1024)}, u32[]{:S(2)}) copy-start(f32[3072]{0:T(1024)} %param.18) | copy-start | bytes 36868
  51.7 14.8 %copy-start.5 = (f32[3072]{0:T(1024)S(1)}, f32[3072]{0:T(1024)}, u32[]{:S(2)}) copy-start(f32[3072]{0:T(1024)} %param.19) | copy-start | bytes 36868
  52.8 13.7 %copy-start.1 = (bf16[256,384]{1,0:T(8,128)(2,1)S(1)}, bf16[256,384]{1,0:T(8,128)(2,1)}, u32[]{:S(2)}) copy-start(bf16[256,384]{1,0:T(8,128)(2,1)} %c0_ref.1) | copy-start | bytes 589828
  52.8 13.7 %copy-start.2 = (bf16[256,384]{1,0:T(8,128)(2,1)S(1)}, bf16[256,384]{1,0:T(8,128)(2,1)}, u32[]{:S(2)}) copy-start(bf16[256,384]{1,0:T(8,128)(2,1)} %c1_ref.1) | copy-start | bytes 589828

commit v6 on v5

--- a/solution.py
+++ b/solution.py
@@ -78,6 +78,8 @@
     high = (sizes >> 8).astype(F32).astype(BF16)
     starts = lax.dot_general(strict, low, NT, preferred_element_type=F32)
     starts = starts + 256.0 * lax.dot_general(strict, high, NT, preferred_element_type=F32)
+    starts = starts.astype(I32).astype(jnp.int16)
+    ranks = rank_ref[...].astype(jnp.int16)
     owned = [
         jnp.where(iota((GROUPS, clusters), 0) == owner_ref[h : h + 1, :], 1.0, 0.0)
         for h in range(heads)
@@ -90,7 +92,7 @@
         label = jnp.where(iota((8, clusters), 0) - 4 * (h % 2) == nth.astype(I32), 1.0, 0.0)
         table = jnp.concatenate([owned[h], label], axis=0)
         step = table - jnp.where(first, 0.0, pltpu.roll(table, 1, 1))
-        reached = ones_where(starts[:, h : h + 1] <= rank_ref[h : h + 1, :].astype(F32))
+        reached = one_hot(starts[:, h : h + 1] <= ranks[h : h + 1, :])
         rows = matmul(step.astype(BF16), reached)
         dests.append(rows[:GROUPS])
         labels.append(rows[GROUPS:])
@@ -193,7 +195,7 @@
     back_ref[:, 8:16, :] = last.astype(BF16)
 
 
-def finish_kernel(back_ref, row_ref, un_ref, att_ref, guided_ref):
+def finish_kernel(parity_ref, back_ref, row_ref, un_ref, att_ref, guided_ref):
     tokens = row_ref.shape[1]
     rows = back_ref.shape[0]
     wide = 2 * HEAD_DIM
@@ -201,9 +203,19 @@
     row = table.astype(I32).astype(jnp.int16)
     pos = iota((tokens, rows), 1).astype(jnp.int16)
     kept = back_ref[...]
+    quarter = iota((rows // 24, 24, wide), 1) >> 2
+    own = quarter == 2 - 2 * parity_ref[0]
+    own = (own | (quarter == 5 - 2 * parity_ref[0])).reshape(rows, wide)
+    apart = kept.astype(F32)
+    apart = jnp.concatenate([jnp.where(own, 0.0, apart), jnp.where(own, apart, 0.0)], axis=1)
+    apart = apart.astype(BF16)
     left = iota((tokens, wide), 1) < HEAD_DIM
+    hits = [row[:, h : h + 1] == pos for h in range(6)]
+    both = [matmul(one_hot(hits[h] | hits[h + 4]), apart) for h in range(2)]
+    found = [x[:, :wide] for x in both] + [matmul(one_hot(hits[h]), kept) for h in (2, 3)]
+    found += [x[:, wide:] for x in both]
     for j in range(3):
-        low, high = (matmul(one_hot(row[:, h : h + 1] == pos), kept) for h in (2 * j, 2 * j + 1))
+        low, high = found[2 * j], found[2 * j + 1]
         if j == 0:
             high = swap_halves(high)
         elif j == 1:
@@ -231,6 +243,16 @@
         copies[-1].start()
 
     send(att_ref, outs[1])
+    chunk = att_ref.shape[0] // 4
+    for start in range(0, att_ref.shape[0], chunk):
+        rows = slice(start, start + chunk)
+        first = (att_ref[rows].astype(F32) - c0_ref[rows].astype(F32)) * 0.5
+        second = (first - c1_ref[rows].astype(F32)) * 0.5
+        third = (second - c2_ref[rows].astype(F32)) * 0.5
+        for i, term in enumerate((first, second, third)):
+            buffers[1 + i][rows] = term.astype(BF16)
+    for i in range(3):
+        send(buffers[1 + i], outs[2 + i])
     parts, _, width = rows_ref.shape
     total = parts * width
     blocks = [rows_ref[i].astype(F32) for i in range(parts)]
@@ -242,16 +264,6 @@
         cols = slice(width * HEAD_ORDER[i], width * (HEAD_ORDER[i] + 1))
         buffers[0][:, cols] = (b * scale * gain_ref[:, cols] + bias_ref[:, cols]).astype(BF16)
     send(buffers[0], outs[0])
-    chunk = att_ref.shape[0] // 4
-    for start in range(0, att_ref.shape[0], chunk):
-        rows = slice(start, start + chunk)
-        first = (att_ref[rows].astype(F32) - c0_ref[rows].astype(F32)) * 0.5
-        second = (first - c1_ref[rows].astype(F32)) * 0.5
-        third = (second - c2_ref[rows].astype(F32)) * 0.5
-        for i, term in enumerate((first, second, third)):
-            buffers[1 + i][rows] = term.astype(BF16)
-    for i in range(3):
-        send(buffers[1 + i], outs[2 + i])
     for copy in copies:
         copy.wait()
 
@@ -287,10 +299,10 @@
     return back.reshape(GROUPS, 3, 4, 128)
 
 
-def finish(back, table, un, **kw):
+def finish(parity, back, table, un, **kw):
     outs = [pltpu.VMEM(un.shape, BF16), pltpu.VMEM((8, un.shape[0] // 8, un.shape[1]), BF16)]
     args = [in_vmem(x) for x in (back.reshape(GROUPS * 12, 128), table, un)]
-    return call(finish_kernel, outs, [VMEM] * 3, *args, **kw)
+    return call(finish_kernel, outs, [SMEM] + [VMEM] * 3, parity, *args, **kw)
 
 
 def last(rows, gain, bias, att, c0, c1, c2, **kw):
@@ -317,7 +329,7 @@
     send, table = pack(parity, qkv, rank, sizes, owner)
     arrived = exchange(send, "tok", TOK_ORDER)
     back = exchange(attend(arrived), "tok", TOK_ORDER)
-    att, guided = finish(back, table, un)
+    att, guided = finish(parity, back, table, un)
     rows = exchange(guided, "head", HEAD_ORDER)
     return tuple(last(rows, gain, bias, att, c0, c1, c2))
 

time: 68 us -> 67.5 us (level)
  no operation moved by 1% of the time
where the time goes in v6:
time: 67.5 us; the launch traced here: 67.3 us
  blocking collectives  60.8 us (90%)
  Pallas kernels  5.76 us (9%)
  between operations  0.71 us (1%)
    all_to_all x3, blocking collectives, exchange(): return lax.all_to_all(x, axis, 0, 0, axis_index_groups=[order], tiled=True)  60.8 us
    pallas_call x3, Pallas kernels, call(): pl.pallas_call(kernel, out_shape=outs, in_specs=in_specs, out_specs=[VMEM...  4.6 us

profile of v6, /device:TPU:6, one launch (start us, length us, event | category | flops | bytes accessed | tf_op | source)
XLA Modules:
  0.0 67.3 jit_solution(15376511675140491630)
XLA Ops:
  0.6 2.3 %shard_map.137 = (bf16[64,40,128]{2,1,0:T(8,128)(2,1)S(1)}, f32[8,256]{1,0:T(8,128)S(1)}) custom-call(s32[1]{0:T(128)} %bitcast.parity_ref, bf16[3,256,384]{2,1,0:T(8,128)(2,1)} %qkv_hbm.1, s32[6,256]{1,0:T(8,128)} %rank_hbm.1, s32[6,256]{1,0:T(8,128)} %sizes_hbm.1, s32[6,256]{1,0:T(8,128)} %owner_hbm.1), custom_call_target="tpu_custom_call" | custom-call | tf_op jit(solution)/shard_map/pallas_call | solution.py:281
  2.9 31.0 %all_to_all.15.recv_ref = bf16[64,40,128]{2,1,0:T(8,128)(2,1)S(1)} all-to-all(bf16[64,40,128]{2,1,0:T(8,128)(2,1)S(1)} %get-tuple-element.9), channel_id=1, replica_groups={{360,488,104,232,376,504,120,248,264,392,8,136,280,408,24,152,296,424,4..., dimensions={0} | all-to-all | bytes 1310720 | tf_op jit(solution)/shard_map/all_to_all | solution.py:324
  33.9 1.6 %shard_map.138 = bf16[32,24,128]{2,1,0:T(8,128)(2,1)S(1)} custom-call(bf16[64,40,128]{2,1,0:T(8,128)(2,1)S(1)} %all_to_all.15.recv_ref), custom_call_target="tpu_custom_call" | custom-call | tf_op jit(solution)/shard_map/pallas_call | solution.py:281
  35.5 0.0 copy-start
  35.5 16.1 %all_to_all.16 = bf16[64,3,4,128]{3,2,1,0:T(4,128)(2,1)S(1)} all-to-all(bf16[64,3,4,128]{3,2,1,0:T(4,128)(2,1)S(1)} %bitcast.6), channel_id=1, replica_groups={{360,488,104,232,376,504,120,248,264,392,8,136,280,408,24,152,296,424,4..., dimensions={0} | all-to-all | bytes 393216 | tf_op jit(solution)/shard_map/all_to_all | solution.py:324
  51.6 0.0 copy-done
  51.6 0.0 copy-start.3
  51.6 0.0 copy-start.4
  51.6 0.0 copy-start.5
  51.6 0.7 %shard_map.139 = (bf16[256,384]{1,0:T(8,128)(2,1)S(1)}, bf16[8,32,384]{2,1,0:T(8,128)(2,1)S(1)}) custom-call(s32[1]{0:T(128)} %bitcast.parity_ref, bf16[768,128]{1,0:T(8,128)(2,1)S(1)} %bitcast.5, f32[8,256]{1,0:T(8,128)S(1)} %get-tuple-element.10.row_ref, bf16[256,384]{1,0:T(8,128)(2,1)S(1)} %copy-done), custom_call_target="tpu_custom_call" | custom-call | tf_op jit(solution)/shard_map/pallas_call | solution.py:281
  52.4 0.0 copy-start.1
  52.4 0.0 copy-start.2
  52.4 13.7 %all_to_all.17.rows_ref = bf16[8,32,384]{2,1,0:T(8,128)(2,1)S(1)} all-to-all(bf16[8,32,384]{2,1,0:T(8,128)(2,1)S(1)} %get-tuple-element.11), channel_id=1, replica_groups={{5,1,6,2,7,3,0,4},{13,9,14,10,15,11,8,12},{21,17,22,18,23,19,16,20},{29..., dimensions={0} | all-to-all | bytes 393216 | tf_op jit(solution)/shard_map/all_to_all | solution.py:324
  66.1 0.0 copy-done.3
  66.1 0.0 copy-done.4
  66.1 0.0 copy-done.5
  66.1 0.0 copy-done.1
  66.1 0.0 copy-done.2
  66.1 1.2 %shard_map.140 = (bf16[32,3072]{1,0:T(8,128)(2,1)}, bf16[256,384]{1,0:T(8,128)(2,1)}, bf16[256,384]{1,0:T(8,128)(2,1)}, bf16[256,384]{1,0:T(8,128)(2,1)}, bf16[256,384]{1,0:T(8,128)(2,1)}) custom-call(bf16[8,32,384]{2,1,0:T(8,128)(2,1)S(1)} %all_to_all.17.rows_ref, f32[1,3072]{1,0:T(1,128)S(1)} %bitcast.7, f32[1,3072]{1,0:T(1,128)S(1)} %bitcast.8, ...), custom_call_target="tpu_custom_call" | custom-call | tf_op jit(solution)/shard_map/pallas_call | solution.py:312
Async XLA Ops:
  35.5 16.2 %copy-start = (bf16[256,384]{1,0:T(8,128)(2,1)S(1)}, bf16[256,384]{1,0:T(8,128)(2,1)}, u32[]{:S(2)}) copy-start(bf16[256,384]{1,0:T(8,128)(2,1)} %un_ref.1) | copy-start | bytes 589828
  51.6 14.5 %copy-start.3 = (bf16[256,384]{1,0:T(8,128)(2,1)S(1)}, bf16[256,384]{1,0:T(8,128)(2,1)}, u32[]{:S(2)}) copy-start(bf16[256,384]{1,0:T(8,128)(2,1)} %c2_ref.1) | copy-start | bytes 589828
  51.6 14.5 %copy-start.4 = (f32[3072]{0:T(1024)S(1)}, f32[3072]{0:T(1024)}, u32[]{:S(2)}) copy-start(f32[3072]{0:T(1024)} %param.18) | copy-start | bytes 36868
  51.6 14.5 %copy-start.5 = (f32[3072]{0:T(1024)S(1)}, f32[3072]{0:T(1024)}, u32[]{:S(2)}) copy-start(f32[3072]{0:T(1024)} %param.19) | copy-start | bytes 36868
  52.4 13.7 %copy-start.1 = (bf16[256,384]{1,0:T(8,128)(2,1)S(1)}, bf16[256,384]{1,0:T(8,128)(2,1)}, u32[]{:S(2)}) copy-start(bf16[256,384]{1,0:T(8,128)(2,1)} %c0_ref.1) | copy-start | bytes 589828
  52.4 13.7 %copy-start.2 = (bf16[256,384]{1,0:T(8,128)(2,1)S(1)}, bf16[256,384]{1,0:T(8,128)(2,1)}, u32[]{:S(2)}) copy-start(bf16[256,384]{1,0:T(8,128)(2,1)} %c1_ref.1) | copy-start | bytes 589828

commit v7 on v6

--- a/solution.py
+++ b/solution.py
@@ -98,7 +98,7 @@
         labels.append(rows[GROUPS:])
     earlier = matmul(jnp.concatenate(dests, axis=0).astype(BF16), before)
     group_id = iota((GROUPS, 1), 0).astype(F32) * float(PAIR_ROWS)
-    slot_rows, places = [], []
+    slot_rows = []
     for h in range(heads):
         offset = group_id
         if h % 2:
@@ -106,7 +106,6 @@
         ahead = earlier[GROUPS * h : GROUPS * (h + 1)] + offset
         slot = jnp.sum(dests[h] * ahead, axis=0, keepdims=True)
         slot_rows.append(slot)
-        places.append(one_hot(slots_iota == slot.astype(I32).astype(jnp.int16)))
     slot = jnp.concatenate(slot_rows, axis=0).astype(I32)
     group, place = slot >> 3, slot & 7
     mixed_row = 12 * group + 4 * parity_ref[0] + place
@@ -130,7 +129,13 @@
         qs, ks, vs = swap_halves(q), swap_halves(k), swap_halves(v)
         even = jnp.concatenate([jnp.where(left, q, ks), jnp.where(left, v, even)], axis=1)
         odd = jnp.concatenate([jnp.where(left, qs, k), jnp.where(left, vs, odd)], axis=1)
-        place = jnp.concatenate(places[2 * j : 2 * j + 2], axis=1)
+        place = jnp.concatenate(
+            [
+                one_hot(slots_iota == slot_rows[h].astype(I32).astype(jnp.int16))
+                for h in (2 * j, 2 * j + 1)
+            ],
+            axis=1,
+        )
         sorted_rows = matmul(place, jnp.concatenate([even, odd], axis=0).astype(BF16))
         send_ref[:, 8 * j : 8 * (j + 1), :] = (
             sorted_rows[:, : 2 * HEAD_DIM].reshape(GROUPS, 8, 2 * HEAD_DIM).astype(BF16)

time: 67.5 us -> 67.5 us (level)
  no operation moved by 1% of the time
where the time goes in v7:
time: 67.5 us; the launch traced here: 67.3 us
  blocking collectives  60.8 us (90%)
  Pallas kernels  5.75 us (9%)
  between operations  0.71 us (1%)
    all_to_all x3, blocking collectives, exchange(): return lax.all_to_all(x, axis, 0, 0, axis_index_groups=[order], tiled=True)  60.8 us
    pallas_call x3, Pallas kernels, call(): pl.pallas_call(kernel, out_shape=outs, in_specs=in_specs, out_specs=[VMEM...  4.59 us

profile of v7, /device:TPU:6, one launch (start us, length us, event | category | flops | bytes accessed | tf_op | source)
XLA Modules:
  0.0 67.3 jit_solution(11669957314941524605)
XLA Ops:
  0.6 2.3 %shard_map.137 = (bf16[64,40,128]{2,1,0:T(8,128)(2,1)S(1)}, f32[8,256]{1,0:T(8,128)S(1)}) custom-call(s32[1]{0:T(128)} %bitcast.parity_ref, bf16[3,256,384]{2,1,0:T(8,128)(2,1)} %qkv_hbm.1, s32[6,256]{1,0:T(8,128)} %rank_hbm.1, s32[6,256]{1,0:T(8,128)} %sizes_hbm.1, s32[6,256]{1,0:T(8,128)} %owner_hbm.1), custom_call_target="tpu_custom_call" | custom-call | tf_op jit(solution)/shard_map/pallas_call | solution.py:286
  2.9 31.0 %all_to_all.15.recv_ref = bf16[64,40,128]{2,1,0:T(8,128)(2,1)S(1)} all-to-all(bf16[64,40,128]{2,1,0:T(8,128)(2,1)S(1)} %get-tuple-element.9), channel_id=1, replica_groups={{360,488,104,232,376,504,120,248,264,392,8,136,280,408,24,152,296,424,4..., dimensions={0} | all-to-all | bytes 1310720 | tf_op jit(solution)/shard_map/all_to_all | solution.py:329
  33.9 1.6 %shard_map.138 = bf16[32,24,128]{2,1,0:T(8,128)(2,1)S(1)} custom-call(bf16[64,40,128]{2,1,0:T(8,128)(2,1)S(1)} %all_to_all.15.recv_ref), custom_call_target="tpu_custom_call" | custom-call | tf_op jit(solution)/shard_map/pallas_call | solution.py:286
  35.5 0.0 copy-start
  35.5 16.1 %all_to_all.16 = bf16[64,3,4,128]{3,2,1,0:T(4,128)(2,1)S(1)} all-to-all(bf16[64,3,4,128]{3,2,1,0:T(4,128)(2,1)S(1)} %bitcast.6), channel_id=1, replica_groups={{360,488,104,232,376,504,120,248,264,392,8,136,280,408,24,152,296,424,4..., dimensions={0} | all-to-all | bytes 393216 | tf_op jit(solution)/shard_map/all_to_all | solution.py:329
  51.6 0.0 copy-done
  51.6 0.0 copy-start.3
  51.6 0.0 copy-start.4
  51.6 0.0 copy-start.5
  51.6 0.7 %shard_map.139 = (bf16[256,384]{1,0:T(8,128)(2,1)S(1)}, bf16[8,32,384]{2,1,0:T(8,128)(2,1)S(1)}) custom-call(s32[1]{0:T(128)} %bitcast.parity_ref, bf16[768,128]{1,0:T(8,128)(2,1)S(1)} %bitcast.5, f32[8,256]{1,0:T(8,128)S(1)} %get-tuple-element.10.row_ref, bf16[256,384]{1,0:T(8,128)(2,1)S(1)} %copy-done), custom_call_target="tpu_custom_call" | custom-call | tf_op jit(solution)/shard_map/pallas_call | solution.py:286
  52.4 0.0 copy-start.1
  52.4 0.0 copy-start.2
  52.4 13.7 %all_to_all.17.rows_ref = bf16[8,32,384]{2,1,0:T(8,128)(2,1)S(1)} all-to-all(bf16[8,32,384]{2,1,0:T(8,128)(2,1)S(1)} %get-tuple-element.11), channel_id=1, replica_groups={{5,1,6,2,7,3,0,4},{13,9,14,10,15,11,8,12},{21,17,22,18,23,19,16,20},{29..., dimensions={0} | all-to-all | bytes 393216 | tf_op jit(solution)/shard_map/all_to_all | solution.py:329
  66.1 0.0 copy-done.3
  66.1 0.0 copy-done.4
  66.1 0.0 copy-done.5
  66.1 0.0 copy-done.1
  66.1 0.0 copy-done.2
  66.1 1.2 %shard_map.140 = (bf16[32,3072]{1,0:T(8,128)(2,1)}, bf16[256,384]{1,0:T(8,128)(2,1)}, bf16[256,384]{1,0:T(8,128)(2,1)}, bf16[256,384]{1,0:T(8,128)(2,1)}, bf16[256,384]{1,0:T(8,128)(2,1)}) custom-call(bf16[8,32,384]{2,1,0:T(8,128)(2,1)S(1)} %all_to_all.17.rows_ref, f32[1,3072]{1,0:T(1,128)S(1)} %bitcast.7, f32[1,3072]{1,0:T(1,128)S(1)} %bitcast.8, ...), custom_call_target="tpu_custom_call" | custom-call | tf_op jit(solution)/shard_map/pallas_call | solution.py:317
Async XLA Ops:
  35.5 16.2 %copy-start = (bf16[256,384]{1,0:T(8,128)(2,1)S(1)}, bf16[256,384]{1,0:T(8,128)(2,1)}, u32[]{:S(2)}) copy-start(bf16[256,384]{1,0:T(8,128)(2,1)} %un_ref.1) | copy-start | bytes 589828
  51.6 14.5 %copy-start.3 = (bf16[256,384]{1,0:T(8,128)(2,1)S(1)}, bf16[256,384]{1,0:T(8,128)(2,1)}, u32[]{:S(2)}) copy-start(bf16[256,384]{1,0:T(8,128)(2,1)} %c2_ref.1) | copy-start | bytes 589828
  51.6 14.5 %copy-start.4 = (f32[3072]{0:T(1024)S(1)}, f32[3072]{0:T(1024)}, u32[]{:S(2)}) copy-start(f32[3072]{0:T(1024)} %param.18) | copy-start | bytes 36868
  51.6 14.5 %copy-start.5 = (f32[3072]{0:T(1024)S(1)}, f32[3072]{0:T(1024)}, u32[]{:S(2)}) copy-start(f32[3072]{0:T(1024)} %param.19) | copy-start | bytes 36868
  52.4 13.7 %copy-start.1 = (bf16[256,384]{1,0:T(8,128)(2,1)S(1)}, bf16[256,384]{1,0:T(8,128)(2,1)}, u32[]{:S(2)}) copy-start(bf16[256,384]{1,0:T(8,128)(2,1)} %c0_ref.1) | copy-start | bytes 589828
  52.4 13.7 %copy-start.2 = (bf16[256,384]{1,0:T(8,128)(2,1)S(1)}, bf16[256,384]{1,0:T(8,128)(2,1)}, u32[]{:S(2)}) copy-start(bf16[256,384]{1,0:T(8,128)(2,1)} %c1_ref.1) | copy-start | bytes 589828

commit v8 on v6

--- a/solution.py
+++ b/solution.py
@@ -9,7 +9,7 @@
 
 HEAD_DIM = 64
 TOK_ORDER = [
-    (16 * (x % 4)) + 2 * (z % 8) + core for core in (1, 0) for z in range(6, 14) for x in range(2, 6)
+    (16 * (x % 4)) + 2 * (z % 8) + core for core in (1, 0) for z in range(6, 14) for x in range(3, 7)
 ]
 HEAD_ORDER = [5, 1, 6, 2, 7, 3, 0, 4]
 GROUPS = 64
@@ -325,7 +325,7 @@
 
 
 def on_device(qkv, rank, sizes, owner, c0, c1, c2, un, gain, bias):
-    parity = ((lax.axis_index("tok") >> 4) & 1).reshape(1)
+    parity = (((lax.axis_index("tok") >> 4) + 1) & 1).reshape(1)
     send, table = pack(parity, qkv, rank, sizes, owner)
     arrived = exchange(send, "tok", TOK_ORDER)
     back = exchange(attend(arrived), "tok", TOK_ORDER)

time: 67.5 us -> 69.4 us (1.028)
  the two profiles are of different devices: /device:TPU:6 before, /device:TPU:1 now
where the time goes in v8:
time: 69.4 us; the launch traced here: 69.2 us
  blocking collectives  62.7 us (90%)
  Pallas kernels  5.75 us (8%)
  between operations  0.71 us (1%)
    all_to_all x3, blocking collectives, exchange(): return lax.all_to_all(x, axis, 0, 0, axis_index_groups=[order], tiled=True)  62.7 us
    pallas_call x3, Pallas kernels, call(): pl.pallas_call(kernel, out_shape=outs, in_specs=in_specs, out_specs=[VMEM...  4.59 us

profile of v8, /device:TPU:1, one launch (start us, length us, event | category | flops | bytes accessed | tf_op | source)
XLA Modules:
  0.0 69.2 jit_solution(11897568739456488929)
XLA Ops:
  0.6 2.3 %shard_map.137 = (bf16[64,40,128]{2,1,0:T(8,128)(2,1)S(1)}, f32[8,256]{1,0:T(8,128)S(1)}) custom-call(s32[1]{0:T(128)} %bitcast.parity_ref, bf16[3,256,384]{2,1,0:T(8,128)(2,1)} %qkv_hbm.1, s32[6,256]{1,0:T(8,128)} %rank_hbm.1, s32[6,256]{1,0:T(8,128)} %sizes_hbm.1, s32[6,256]{1,0:T(8,128)} %owner_hbm.1), custom_call_target="tpu_custom_call" | custom-call | tf_op jit(solution)/shard_map/pallas_call | solution.py:281
  2.9 33.1 %all_to_all.15.recv_ref = bf16[64,40,128]{2,1,0:T(8,128)(2,1)S(1)} all-to-all(bf16[64,40,128]{2,1,0:T(8,128)(2,1)S(1)} %get-tuple-element.9), channel_id=1, replica_groups={{488,104,232,360,504,120,248,376,392,8,136,264,408,24,152,280,424,40,16..., dimensions={0} | all-to-all | bytes 1310720 | tf_op jit(solution)/shard_map/all_to_all | solution.py:324
  36.0 1.6 %shard_map.138 = bf16[32,24,128]{2,1,0:T(8,128)(2,1)S(1)} custom-call(bf16[64,40,128]{2,1,0:T(8,128)(2,1)S(1)} %all_to_all.15.recv_ref), custom_call_target="tpu_custom_call" | custom-call | tf_op jit(solution)/shard_map/pallas_call | solution.py:281
  37.6 0.0 copy-start
  37.6 16.6 %all_to_all.16 = bf16[64,3,4,128]{3,2,1,0:T(4,128)(2,1)S(1)} all-to-all(bf16[64,3,4,128]{3,2,1,0:T(4,128)(2,1)S(1)} %bitcast.6), channel_id=1, replica_groups={{488,104,232,360,504,120,248,376,392,8,136,264,408,24,152,280,424,40,16..., dimensions={0} | all-to-all | bytes 393216 | tf_op jit(solution)/shard_map/all_to_all | solution.py:324
  54.2 0.0 copy-done
  54.2 0.0 copy-start.3
  54.2 0.0 copy-start.4
  54.2 0.0 copy-start.5
  54.2 0.7 %shard_map.139 = (bf16[256,384]{1,0:T(8,128)(2,1)S(1)}, bf16[8,32,384]{2,1,0:T(8,128)(2,1)S(1)}) custom-call(s32[1]{0:T(128)} %bitcast.parity_ref, bf16[768,128]{1,0:T(8,128)(2,1)S(1)} %bitcast.5, f32[8,256]{1,0:T(8,128)S(1)} %get-tuple-element.10.row_ref, bf16[256,384]{1,0:T(8,128)(2,1)S(1)} %copy-done), custom_call_target="tpu_custom_call" | custom-call | tf_op jit(solution)/shard_map/pallas_call | solution.py:281
  55.0 0.0 copy-start.1
  55.0 0.0 copy-start.2
  55.0 13.0 %all_to_all.17.rows_ref = bf16[8,32,384]{2,1,0:T(8,128)(2,1)S(1)} all-to-all(bf16[8,32,384]{2,1,0:T(8,128)(2,1)S(1)} %get-tuple-element.11), channel_id=1, replica_groups={{5,1,6,2,7,3,0,4},{13,9,14,10,15,11,8,12},{21,17,22,18,23,19,16,20},{29..., dimensions={0} | all-to-all | bytes 393216 | tf_op jit(solution)/shard_map/all_to_all | solution.py:324
  68.0 0.0 copy-done.3
  68.0 0.0 copy-done.4
  68.0 0.0 copy-done.5
  68.0 0.0 copy-done.1
  68.0 0.0 copy-done.2
  68.0 1.2 %shard_map.140 = (bf16[32,3072]{1,0:T(8,128)(2,1)}, bf16[256,384]{1,0:T(8,128)(2,1)}, bf16[256,384]{1,0:T(8,128)(2,1)}, bf16[256,384]{1,0:T(8,128)(2,1)}, bf16[256,384]{1,0:T(8,128)(2,1)}) custom-call(bf16[8,32,384]{2,1,0:T(8,128)(2,1)S(1)} %all_to_all.17.rows_ref, f32[1,3072]{1,0:T(1,128)S(1)} %bitcast.7, f32[1,3072]{1,0:T(1,128)S(1)} %bitcast.8, ...), custom_call_target="tpu_custom_call" | custom-call | tf_op jit(solution)/shard_map/pallas_call | solution.py:312
Async XLA Ops:
  37.6 16.6 %copy-start = (bf16[256,384]{1,0:T(8,128)(2,1)S(1)}, bf16[256,384]{1,0:T(8,128)(2,1)}, u32[]{:S(2)}) copy-start(bf16[256,384]{1,0:T(8,128)(2,1)} %un_ref.1) | copy-start | bytes 589828
  54.2 13.8 %copy-start.3 = (bf16[256,384]{1,0:T(8,128)(2,1)S(1)}, bf16[256,384]{1,0:T(8,128)(2,1)}, u32[]{:S(2)}) copy-start(bf16[256,384]{1,0:T(8,128)(2,1)} %c2_ref.1) | copy-start | bytes 589828
  54.2 13.8 %copy-start.4 = (f32[3072]{0:T(1024)S(1)}, f32[3072]{0:T(1024)}, u32[]{:S(2)}) copy-start(f32[3072]{0:T(1024)} %param.18) | copy-start | bytes 36868
  54.2 13.8 %copy-start.5 = (f32[3072]{0:T(1024)S(1)}, f32[3072]{0:T(1024)}, u32[]{:S(2)}) copy-start(f32[3072]{0:T(1024)} %param.19) | copy-start | bytes 36868
  55.0 13.0 %copy-start.1 = (bf16[256,384]{1,0:T(8,128)(2,1)S(1)}, bf16[256,384]{1,0:T(8,128)(2,1)}, u32[]{:S(2)}) copy-start(bf16[256,384]{1,0:T(8,128)(2,1)} %c0_ref.1) | copy-start | bytes 589828
  55.0 13.0 %copy-start.2 = (bf16[256,384]{1,0:T(8,128)(2,1)S(1)}, bf16[256,384]{1,0:T(8,128)(2,1)}, u32[]{:S(2)}) copy-start(bf16[256,384]{1,0:T(8,128)(2,1)} %c1_ref.1) | copy-start | bytes 589828
